TPU v7x, 128 devices: a whole 4x4x4 slice. The times are simulated.
128 devices in a mesh: pipe: 8 (over x, z_hi), tensor: 16 (over z_lo, y, core).
Axes of the slice: x: 4, y: 4, z: 4 (z_hi: 2, z_lo: 2; z = z_hi * 2 + z_lo), core: 2. Of those that a mesh axis runs over, the one named last changes fastest.
Arguments:
- layer_input: bfloat16 [768, 8192], P('tensor', 'pipe'), may hold values from -6 to 6
- out_grad: bfloat16 [768, 8192], P('tensor', 'pipe'), may hold values from -2 to 2
- gate_pre: bfloat16 [768, 28672], P(None, 'tensor'), may hold values from -8 to 8
- up_pre: bfloat16 [768, 28672], P(None, 'tensor'), may hold values from -6 to 6
- gate_weight: bfloat16 [8192, 28672], P('pipe', 'tensor'), may hold values from -0.0625 to 0.0625
- up_weight: bfloat16 [8192, 28672], P('pipe', 'tensor'), may hold values from -0.0625 to 0.0625
- down_weight: bfloat16 [28672, 8192], P('tensor', 'pipe'), may hold values from -0.03125 to 0.03125
- gate_mask: int32 [64, 224], P('pipe', 'tensor'), may hold values from 0 to 1, as said below
- up_mask: int32 [64, 224], P('pipe', 'tensor'), may hold values from 0 to 1, as said below
- down_mask: int32 [224, 64], P('tensor', 'pipe'), may hold values from 0 to 1, as said below
Outputs:
- grad_input: bfloat16 [768, 8192], P('tensor', 'pipe')
- grad_gate: bfloat16 [8192, 28672], P('pipe', 'tensor')
- grad_up: bfloat16 [8192, 28672], P('pipe', 'tensor')
- grad_down: bfloat16 [28672, 8192], P('tensor', 'pipe')
Inputs may be any that keep to these rules, and one draw needn't show every extreme that they name: `gate_mask`: each entry is 1 for a kept block and 0 for a pruned one; the share of kept blocks differs from block column to block column. `up_mask`: each entry is 1 for a kept block and 0 for a pruned one; the share of kept blocks differs from block column to block column. `down_mask`: each entry is 1 for a kept block and 0 for a pruned one; the share of kept blocks differs from block row to block row.
All inputs are finite; a program needn't handle non-finite values.
Results may differ from a plain program's by a relative error of at most 0.005.
Values may be sent and summed in bfloat16 or wider, within the bound.
A program may use at most 128 MiB of HBM per device.

v0:
```python
import jax
import jax.numpy as jnp
from jax import lax
from jax.sharding import PartitionSpec as P

BLOCK = 128


def expand(mask):
    return jnp.repeat(jnp.repeat(mask, BLOCK, axis=0), BLOCK, axis=1)


def local_grads(hidden_grad, gate_val, up_val, sigma_val):
    gate_grad = (hidden_grad * up_val * sigma_val * (1.0 + gate_val * (1.0 - sigma_val))).astype(
        jnp.bfloat16
    )
    up_grad = (hidden_grad * gate_val * sigma_val).astype(jnp.bfloat16)
    return (gate_grad, up_grad)


def shards(
    layer_input,
    out_grad,
    gate_pre,
    up_pre,
    gate_weight,
    up_weight,
    down_weight,
    gate_mask,
    up_mask,
    down_mask,
):
    mask_gate = expand(gate_mask)
    mask_up = expand(up_mask)
    mask_down = expand(down_mask)
    gate_masked = gate_weight * mask_gate.astype(jnp.bfloat16)
    up_masked = up_weight * mask_up.astype(jnp.bfloat16)
    down_masked = down_weight * mask_down.astype(jnp.bfloat16)
    gate_val = gate_pre.astype(jnp.float32)
    up_val = up_pre.astype(jnp.float32)
    sigma_val = jax.nn.sigmoid(gate_val)
    hidden = (gate_val * sigma_val * up_val).astype(jnp.bfloat16)
    piece = lax.all_gather(out_grad, "tensor", axis=0, tiled=True)
    down_acc = lax.dot_general(
        hidden, piece, (((0,), (0,)), ((), ())), preferred_element_type=jnp.float32
    )
    partial_rows = lax.dot_general(
        piece, down_masked, (((1,), (1,)), ((), ())), preferred_element_type=jnp.float32
    )
    hidden_grad = partial_rows
    down_acc, hidden_partial = (down_acc, hidden_grad)
    grad_down = (down_acc * mask_down.astype(jnp.float32)).astype(jnp.bfloat16)
    hidden_grad = lax.psum(hidden_partial, "pipe")
    gate_grad, up_grad = local_grads(hidden_grad, gate_val, up_val, sigma_val)
    piece = lax.all_gather(layer_input, "tensor", axis=0, tiled=True)
    gate_rows = gate_grad
    up_rows = up_grad
    gate_acc = lax.dot_general(
        piece, gate_rows, (((0,), (0,)), ((), ())), preferred_element_type=jnp.float32
    )
    up_acc = lax.dot_general(
        piece, up_rows, (((0,), (0,)), ((), ())), preferred_element_type=jnp.float32
    )
    gate_acc, up_acc = (gate_acc, up_acc)
    grad_gate = (gate_acc * mask_gate.astype(jnp.float32)).astype(jnp.bfloat16)
    grad_up = (up_acc * mask_up.astype(jnp.float32)).astype(jnp.bfloat16)
    gate_rows = gate_grad
    up_rows = up_grad
    total = lax.dot_general(
        gate_rows, gate_masked, (((1,), (1,)), ((), ())), preferred_element_type=jnp.float32
    )
    grad_input = lax.psum_scatter(
        total
        + lax.dot_general(
            up_rows, up_masked, (((1,), (1,)), ((), ())), preferred_element_type=jnp.float32
        ),
        "tensor",
        scatter_dimension=0,
        tiled=True,
    ).astype(jnp.bfloat16)
    return (grad_input, grad_gate, grad_up, grad_down)


def solution(mesh):
    in_specs = (
        P("tensor", "pipe"),
        P("tensor", "pipe"),
        P(None, "tensor"),
        P(None, "tensor"),
        P("pipe", "tensor"),
        P("pipe", "tensor"),
        P("tensor", "pipe"),
        P("pipe", "tensor"),
        P("pipe", "tensor"),
        P("tensor", "pipe"),
    )
    out_specs = (P("tensor", "pipe"), P("pipe", "tensor"), P("pipe", "tensor"), P("tensor", "pipe"))
    return jax.shard_map(shards, mesh=mesh, in_specs=in_specs, out_specs=out_specs, check_vma=False)
```

profile of v0, /device:TPU:1, one launch (start us, length us, event | category | flops | bytes accessed | tf_op | source)
XLA Modules:
  0.0 400.9 jit_solution(1261620353858778361)
XLA Ops:
  7.9 0.8 fusion.17
  8.8 37.7 %all-gather.3.cloned.1.call-done = bf16[768,1024]{1,0:T(8,128)(2,1)} async-done(((bf16[48,1024]{1,0:T(8,128)(2,1)}), bf16[768,1024]{1,0:T(8,128)(2,1)}) %all-gather.3.cloned.1.call-update) | async-done | bytes 1572880 | tf_op jit(solution)/shard_map/all_gather | solution.py:43
  46.6 5.1 %broadcast_in_dim.31 = bf16[1792,8,128]{2,1,0:T(8,128)(2,1)S(1)} broadcast(bf16[1792,8]{1,0:T(8,128)(2,1)S(1)} %bitcast.66), dimensions={0,1} | broadcast | bytes 3698688 | tf_op jit(solution)/shard_map/broadcast_in_dim | solution.py:10
  51.7 6.4 %convolution_bitcast_fusion = f32[768,1792]{0,1:T(8,128)} fusion(bf16[768,1024]{1,0:T(8,128)(2,1)} %all-gather.3.cloned.1.call-done, bf16[1792,1024]{1,0:T(8,128)(2,1)S(1)} %copy-done.9, bf16[224,8,8,128]{3,2,1,0:T(8,128)(2,1)S(1)} %bitcast.64), kind=kOutput, calls=%fused_computation.22 | convolution fusion | flops 2820407296 | bytes 14417920 | tf_op jit(solution)/shard_map/dot_general | solution.py:47
  59.1 3.3 copy.23
  62.4 4.5 %copy.24 = bf16[768,1792]{0,1:T(8,128)(2,1)} copy(bf16[768,1792]{1,0:T(8,128)(2,1)} %param.12) | data formatting | bytes 5505024 | tf_op args[2]
  67.2 6.0 %copy.26 = bf16[1024,1792]{0,1:T(8,128)(2,1)} copy(bf16[1024,1792]{1,0:T(8,128)(2,1)} %param.14) | data formatting | bytes 7340032 | tf_op args[4]
  73.4 6.0 %copy.28 = bf16[1024,1792]{0,1:T(8,128)(2,1)} copy(bf16[1024,1792]{1,0:T(8,128)(2,1)} %param.15) | data formatting | bytes 7340032 | tf_op args[5]
  79.3 4.3 %bitcast_multiply_fusion.6 = bf16[1024,1792]{0,1:T(8,128)(2,1)} fusion(bf16[1024,1792]{0,1:T(8,128)(2,1)} %copy.26, bf16[1024,14]{0,1:T(8,128)(2,1)S(1)} %bitcast.69), kind=kLoop, calls=%fused_computation.26 | loop fusion | flops 1835008 | bytes 7368704 | tf_op jit(solution)/shard_map/mul | solution.py:36
  83.6 2.1 bitcast_multiply_fusion.5
  85.7 206.9 %all-reduce.2.cloned.1.call-done = f32[768,1792]{0,1:T(8,128)} async-done(((f32[768,1792]{0,1:T(8,128)}), f32[768,1792]{0,1:T(8,128)}) %all-reduce.2.cloned.1.call-update) | async-done | bytes 5505040 | tf_op jit(solution)/shard_map/psum | solution.py:53
  292.6 5.0 %fusion.12 = (bf16[768,1792]{0,1:T(8,128)(2,1)S(1)}, bf16[768,1792]{0,1:T(8,128)(2,1)S(1)}) fusion(f32[768,1792]{0,1:T(8,128)} %all-reduce.2.cloned.1.call-done, bf16[768,1792]{0,1:T(8,128)(2,1)} %copy.24, bf16[768,1792]{0,1:T(8,128)(2,1)S(1)} %copy.23), kind=kLoop, calls=%fused_computation.21 | loop fusion | flops 20643840 | bytes 16515072 | tf_op jit(solution)/shard_map/convert_element_type | solution.py:17
  297.6 3.1 fusion.20
  300.8 0.9 copy-done.1
  301.6 4.9 %convolution_add_fusion = f32[768,1024]{1,0:T(8,128)} fusion(f32[768,1024]{1,0:T(8,128)S(1)} %fusion.20, bf16[768,1792]{0,1:T(8,128)(2,1)S(1)} %get-tuple-element.12, bf16[1024,1792]{0,1:T(8,128)(2,1)S(1)} %copy-done.1), kind=kOutput, calls=%fused_computation.28 | convolution fusion | flops 2819358720 | bytes 12713984 | tf_op jit(solution)/shard_map/dot_general | solution.py:74
  307.2 2.0 broadcast_in_dim.41
  309.4 5.2 %fusion = bf16[1792,1024]{1,0:T(8,128)(2,1)} fusion(f32[224,8,8,128]{3,2,1,0:T(8,128)S(1)} %bitcast.63, bf16[768,1024]{1,0:T(8,128)(2,1)S(1)} %copy-done.10, bf16[768,1792]{0,1:T(8,128)(2,1)S(1)} %copy.23, bf16[768,1792]{0,1:T(8,128)(2,1)S(1)} %copy-done.2), kind=kOutput, calls=%fused_computation.5 | convolution fusion | flops 2833252352 | bytes 18087936 | tf_op jit(solution)/shard_map/dot_general | solution.py:44
  314.6 14.9 %all-gather.5.cloned.1.call-done = bf16[768,1024]{1,0:T(8,128)(2,1)} async-done(((bf16[48,1024]{1,0:T(8,128)(2,1)}), bf16[768,1024]{1,0:T(8,128)(2,1)}) %all-gather.5.cloned.1.call-update) | async-done | bytes 1572880 | tf_op jit(solution)/shard_map/all_gather | solution.py:55
  329.6 7.1 %fusion.2 = bf16[1024,1792]{0,1:T(8,128)(2,1)} fusion(bf16[768,1792]{0,1:T(8,128)(2,1)} %copy-done.6, bf16[768,1024]{1,0:T(8,128)(2,1)} %all-gather.5.cloned.1.call-done, f32[1024,14]{0,1:T(8,128)S(1)} %bitcast.73), kind=kOutput, calls=%fused_computation.9 | convolution fusion | flops 2822242304 | bytes 8052736 | tf_op jit(solution)/shard_map/dot_general | solution.py:58
  336.7 6.1 %copy.32 = bf16[1024,1792]{1,0:T(8,128)(2,1)} copy(bf16[1024,1792]{0,1:T(8,128)(2,1)} %fusion.2) | data formatting | bytes 7340032
  342.7 6.2 %fusion.1 = bf16[1024,1792]{0,1:T(8,128)(2,1)} fusion(bf16[768,1792]{0,1:T(8,128)(2,1)S(1)} %copy-done.4, bf16[768,1024]{1,0:T(8,128)(2,1)} %all-gather.5.cloned.1.call-done, f32[1024,14]{0,1:T(8,128)S(1)} %bitcast.74), kind=kOutput, calls=%fused_computation.7 | convolution fusion | flops 2822242304 | bytes 8052736 | tf_op jit(solution)/shard_map/dot_general | solution.py:61
  349.0 5.9 %copy.33 = bf16[1024,1792]{1,0:T(8,128)(2,1)} copy(bf16[1024,1792]{0,1:T(8,128)(2,1)} %fusion.1) | data formatting | bytes 7340032
  354.9 37.9 %reduce-scatter.2.cloned.1.call-done = f32[48,1024]{1,0:T(8,128)} async-done(((f32[768,1024]{1,0:T(8,128)}), f32[48,1024]{1,0:T(8,128)}) %reduce-scatter.2.cloned.1.call-update) | async-done | bytes 196624 | tf_op jit(solution)/shard_map/reduce_scatter | solution.py:72
  392.8 1.6 convert_element_type.106
  (51 shorter events, 3.0 us)
Async XLA Ops:
  7.2 39.4 %all-gather.3.cloned.1.call-start = ((), (), s32[]{:S(2)}) async-start(), calls=%async_computation.1 | async-start | bytes 1671168 | tf_op jit(solution)/shard_map/all_gather | solution.py:43
  7.9 284.7 %all-reduce.2.cloned.1.call-start = ((), (), s32[]{:S(2)}) async-start(), calls=%async_computation.2 | async-start | bytes 11010048 | tf_op jit(solution)/shard_map/psum | solution.py:53
  46.5 5.2 %copy-start.9 = (bf16[1792,1024]{1,0:T(8,128)(2,1)S(1)}, bf16[1792,1024]{1,0:T(8,128)(2,1)}, u32[]{:S(2)}) copy-start(bf16[1792,1024]{1,0:T(8,128)(2,1)} %param.16) | copy-start | bytes 11010052
  58.1 271.4 %all-gather.5.cloned.1.call-start = ((), (), s32[]{:S(2)}) async-start(), calls=%async_computation.4 | async-start | bytes 1671168 | tf_op jit(solution)/shard_map/all_gather | solution.py:55
  58.9 333.9 %reduce-scatter.2.cloned.1.call-start = ((), (), s32[]{:S(2)}) async-start(), calls=%async_computation.3 | async-start | bytes 3342336 | tf_op jit(solution)/shard_map/reduce_scatter | solution.py:72
  62.4 4.5 %copy-start.7 = (s32[8,14]{1,0:T(8,128)S(1)}, s32[8,14]{1,0:T(8,128)}, u32[]{:S(2)}) copy-start(s32[8,14]{1,0:T(8,128)} %param.17) | copy-start | bytes 1348
  67.2 6.0 %copy-start.8 = (s32[8,14]{1,0:T(8,128)S(1)}, s32[8,14]{1,0:T(8,128)}, u32[]{:S(2)}) copy-start(s32[8,14]{1,0:T(8,128)} %param.18) | copy-start | bytes 1348
  79.3 4.3 %copy-start = (bf16[1024,1792]{0,1:T(8,128)(2,1)S(1)}, bf16[1024,1792]{0,1:T(8,128)(2,1)}, u32[]{:S(2)}) copy-start(bf16[1024,1792]{0,1:T(8,128)(2,1)} %copy.28) | copy-start | bytes 11010052
  292.6 5.1 %copy-start.5 = (bf16[1024,1792]{0,1:T(8,128)(2,1)S(1)}, bf16[1024,1792]{0,1:T(8,128)(2,1)}, u32[]{:S(2)}) copy-start(bf16[1024,1792]{0,1:T(8,128)(2,1)} %bitcast_multiply_fusion.6) | copy-start | bytes 11010052
  297.6 3.1 copy-start.6
  297.6 3.1 copy-start.3
  297.6 4.0 %copy-start.1 = (bf16[1024,1792]{0,1:T(8,128)(2,1)S(1)}, bf16[1024,1792]{0,1:T(8,128)(2,1)}, u32[]{:S(2)}) copy-start(bf16[1024,1792]{0,1:T(8,128)(2,1)} %bitcast_multiply_fusion.5) | copy-start | bytes 11010052
  307.1 2.1 copy-start.2
  307.2 2.3 copy-start.10
  336.7 6.1 %copy-start.4 = (bf16[768,1792]{0,1:T(8,128)(2,1)S(1)}, bf16[768,1792]{0,1:T(8,128)(2,1)}, u32[]{:S(2)}) copy-start(bf16[768,1792]{0,1:T(8,128)(2,1)} %copy-done.3) | copy-start | bytes 8257540
Sparse Core Ops, SparseCore 0:
  9.7 36.7 all-gather.2
  58.2 234.2 all-reduce.1
  294.3 35.2 all-gather.4
  331.8 60.8 reduce-scatter.1
where the time goes:
time: 405 us; the launch traced here: 401 us
  waiting for transfers between devices  299 us (74%)
  local copies, waits for them, and re-layouts  41.1 us (10%)
  matrix products  32.9 us (8%)
  between operations  14 us (3%)
  other arithmetic  13.7 us (3%)
    psum x1, waiting for transfers between devices, shards(): hidden_grad = lax.psum(hidden_partial, 'pipe')  207 us
    reduce_scatter x1, waiting for transfers between devices, shards(): lax.psum_scatter(total + lax.dot_general(up_rows, up_masked, (((1,), (1,)...  37.9 us
    all_gather x1, waiting for transfers between devices, shards(): piece = lax.all_gather(out_grad, 'tensor', axis=0, tiled=True)  37.7 us
    unnamed x40, local copies, waits for them, and re-layouts  33.3 us
    all_gather x1, waiting for transfers between devices, shards(): piece = lax.all_gather(layer_input, 'tensor', axis=0, tiled=True)  14.9 us
  transfers between devices with their start and end apart: 4, of which 4 were waited for; matrix products, arithmetic and copies ran while one was open for 18% of the time, Pallas kernels for 0%

commit v1 on v0

v1 whole, which is shorter than its diff:
```python
import jax
import jax.numpy as jnp
from jax import lax
from jax.experimental import pallas as pl
from jax.experimental.pallas import tpu as pltpu
from jax.sharding import PartitionSpec as P

MESH = pl.DeviceIdType.MESH
BF = jnp.bfloat16
F32 = jnp.float32
ROWS = 48
D = 1024
FF = 1792
NA = 8
NC = 14
GATHER = 15


def coords():
    p, t = lax.axis_index("pipe"), lax.axis_index("tensor")
    return (
        lax.div(p, 2),
        lax.rem(p, 2),
        lax.div(t, 8),
        lax.rem(lax.div(t, 2), 4),
        lax.rem(t, 2),
    )


def device(x, zh, zl, y, c):
    return (lax.rem(x, 4) * 2 + zh, zl * 8 + lax.rem(y, 4) * 2 + c)


def rank(zl, y, c):
    return zl * 8 + lax.rem(y, 4) * 2 + c


class Copies:
    def __init__(self, send, recv):
        self.send, self.recv, self.all = send, recv, []

    def start(self, i, src, dst, dev):
        c = pltpu.make_async_remote_copy(
            src_ref=src,
            dst_ref=dst,
            send_sem=self.send.at[i],
            recv_sem=self.recv.at[i],
            device_id=dev,
            device_id_type=MESH,
        )
        c.start()
        self.all.append(c)
        return c

    def finish(self):
        for c in self.all:
            c.wait_send()


class Gather:
    def __init__(self, cp, base, src, full, sem):
        self.cp, self.base, self.full = cp, base, full
        x, zh, zl, y, c = self.at = coords()
        me = rank(zl, y, c)
        self.own = pltpu.make_async_copy(src, full.at[me], sem)
        self.own.start()
        dst = full.at[me]
        self.z = cp.start(base, src, dst, device(x, zh, 1 - zl, y, c))
        self.y1 = [cp.start(base + k, src, dst, device(x, zh, zl, y + k, c)) for k in (1, 3, 2)]
        self.sib = [cp.start(base + 7, src, dst, device(x, zh, zl, y, 1 - c))]
        self.n = 7

    def to_sibling(self, r):
        x, zh, zl, y, c = self.at
        self.n += 1
        piece = self.full.at[r]
        self.sib.append(self.cp.start(self.base + self.n, piece, piece, device(x, zh, zl, y, 1 - c)))

    def step_z(self):
        x, zh, zl, y, c = self.at
        self.z.wait_recv()
        piece = self.full.at[rank(1 - zl, y, c)]
        self.y2 = [
            self.cp.start(self.base + 3 + k, piece, piece, device(x, zh, zl, y + k, c))
            for k in (1, 3, 2)
        ]
        self.to_sibling(rank(1 - zl, y, c))

    def step_y(self):
        x, zh, zl, y, c = self.at
        for copies, z in ((self.y1, zl), (self.y2, 1 - zl)):
            for copy, k in zip(copies, (1, 3, 2)):
                copy.wait_recv()
                self.to_sibling(rank(z, y + 4 - k, c))

    def finish(self):
        for copy in self.sib:
            copy.wait_recv()
        self.own.wait()


def add(*refs):
    total = refs[0][...].astype(F32)
    for r in refs[1:]:
        total = total + r[...].astype(F32)
    return total


def hidden_kernel(
    mask_ref, x_hbm, og_hbm, dw_hbm,
    hg, x_full, og_full,
    dw, hp, rl1, rl2, rl3, rr1, rr2, rr3, asum, fa, rz,
    rb, bs, bl1, bl2, bl3, br1, br2, br3,
    send, recv, local,
):
    x, zh, zl, y, c = coords()
    right, left = device(x + 1, zh, zl, y, c), device(x + 3, zh, zl, y, c)
    other = device(x, 1 - zh, zl, y, c)
    x1, x2, x3 = lax.rem(x + 1, 4), lax.rem(x + 2, 4), lax.rem(x + 3, 4)

    barrier = pltpu.get_barrier_semaphore()
    partners = [right, left, other, device(x, zh, 1 - zl, y, c), device(x, zh, zl, y, 1 - c)]
    partners += [device(x, zh, zl, y + k, c) for k in (1, 2, 3)]
    load = pltpu.make_async_copy(dw_hbm, dw, local.at[0])
    load.start()
    for d in partners:
        pl.semaphore_signal(barrier, inc=1, device_id=d, device_id_type=MESH)
    pl.semaphore_wait(barrier, len(partners))

    cp = Copies(send, recv)
    og = Gather(cp, 0, og_hbm, og_full, local.at[1])
    load.wait()

    @pl.loop(0, NC)
    def _(i):
        for k in range(D // 128):
            at = (pl.ds(pl.multiple_of(i * 128, 128), 128), pl.ds(k * 128, 128))
            dw[at] = dw[at] * mask_ref[i, k].astype(F32).astype(BF)

    og.step_z()
    og.step_y()
    og.finish()

    def partial(first, last):
        @pl.loop(first // 2, last // 2)
        def _(j):
            w = dw[pl.ds(pl.multiple_of(j * 256, 256), 256), :]
            acc = lax.dot_general(
                og_full[...].reshape(768, D), w, (((1,), (1,)), ((), ())), preferred_element_type=F32
            ).astype(BF)
            hp[2 * j] = acc[:, :128].reshape(2, 4, 96, 128)
            hp[2 * j + 1] = acc[:, 128:].reshape(2, 4, 96, 128)

    L, R, B = pl.ds(0, 4), pl.ds(4, 4), pl.ds(NA, 6)
    BL, BR = pl.ds(0, 3), pl.ds(3, 3)
    s = 2 * GATHER
    partial(NA, NC)
    zb = cp.start(s, hp.at[B, 1 - zh], rb, other)
    partial(0, 4)
    a1r = cp.start(s + 1, hp.at[L, :, x2], rl1, right)
    partial(4, 8)
    a1l = cp.start(s + 2, hp.at[R, :, x2], rr1, left)
    a2r = cp.start(s + 3, hp.at[R, :, x1], rl2, right)
    a2l = cp.start(s + 4, hp.at[L, :, x3], rr2, left)
    inp = Gather(cp, GATHER, x_hbm, x_full, local.at[2])
    a1r.wait_recv()
    rl1[...] = add(rl1, hp.at[L, :, x1]).astype(BF)
    a3r = cp.start(s + 5, rl1, rl3, right)
    a1l.wait_recv()
    rr1[...] = add(rr1, hp.at[R, :, x3]).astype(BF)
    a3l = cp.start(s + 6, rr1, rr3, left)
    inp.step_z()
    zb.wait_recv()
    bs[...] = add(rb, hp.at[B, zh]).astype(BF)
    b1r = cp.start(s + 8, bs.at[BL, x2], bl1, right)
    b1l = cp.start(s + 9, bs.at[BR, x2], br1, left)
    b2r = cp.start(s + 10, bs.at[BR, x1], bl2, right)
    b2l = cp.start(s + 11, bs.at[BL, x3], br2, left)
    inp.step_y()
    for copy in (a2r, a2l, a3r, a3l):
        copy.wait_recv()
    asum[L] = add(hp.at[L, :, x], rl3, rr2)
    asum[R] = add(hp.at[R, :, x], rr3, rl2)
    fa[...] = asum[:, 1 - zh].astype(BF)
    za = cp.start(s + 7, fa, rz, other)
    b1r.wait_recv()
    bl1[...] = add(bl1, bs.at[BL, x1]).astype(BF)
    b3r = cp.start(s + 12, bl1, bl3, right)
    b1l.wait_recv()
    br1[...] = add(br1, bs.at[BR, x3]).astype(BF)
    b3l = cp.start(s + 13, br1, br3, left)
    inp.finish()

    g = s + 14
    A, AL, AR = pl.ds(0, NA), pl.ds(0, 4), pl.ds(4, 4)
    GL, GR = pl.ds(NA, 3), pl.ds(NA + 3, 3)

    def send_rows(i, cols, h, q, dev):
        piece = hg.at[cols, h, q]
        return cp.start(g + i, piece, piece, dev)

    za.wait_recv()
    hg[A, zh, x] = add(asum.at[:, zh], rz).astype(BF)
    ga = send_rows(0, A, zh, x, other)
    gr = [send_rows(1, A, zh, x, right)]
    gl = [send_rows(2, A, zh, x, left)]
    for copy in (b2r, b2l, b3r, b3l):
        copy.wait_recv()
    hg[GL, zh, x] = add(bs.at[BL, x], bl3, br2).astype(BF)
    hg[GR, zh, x] = add(bs.at[BR, x], br3, bl2).astype(BF)
    br = send_rows(9, B, zh, x, right)
    bl = send_rows(10, B, zh, x, left)
    z = [send_rows(13, B, zh, x, other)]
    ga.wait_recv()
    gr.append(send_rows(3, A, 1 - zh, x, right))
    gl.append(send_rows(4, A, 1 - zh, x, left))
    br.wait_recv()
    fr = send_rows(11, GL, zh, x3, right)
    z.append(send_rows(14, B, zh, x3, other))
    bl.wait_recv()
    fl = send_rows(12, GR, zh, x1, left)
    z.append(send_rows(15, B, zh, x1, other))
    f = []
    gr[0].wait_recv()
    f.append(send_rows(5, AL, zh, x3, right))
    gl[0].wait_recv()
    f.append(send_rows(6, AR, zh, x1, left))
    fr.wait_recv()
    z.append(send_rows(16, GL, zh, x2, other))
    fl.wait_recv()
    z.append(send_rows(17, GR, zh, x2, other))
    gr[1].wait_recv()
    f.append(send_rows(7, AL, 1 - zh, x3, right))
    gl[1].wait_recv()
    f.append(send_rows(8, AR, 1 - zh, x1, left))
    for copy in f + z:
        copy.wait_recv()
    cp.finish()


def hidden_gradient(down_mask, layer_input, out_grad, down_weight):
    vmem = pl.BlockSpec(memory_space=pltpu.VMEM)
    hbm = pl.BlockSpec(memory_space=pl.ANY)
    a = pltpu.VMEM((4, 2, 96, 128), BF)
    b = pltpu.VMEM((3, 96, 128), BF)
    copies = 2 * GATHER + 14 + 18
    return pl.pallas_call(
        hidden_kernel,
        name="hidden_gradient",
        out_shape=(
            jax.ShapeDtypeStruct((NC, 2, 4, 96, 128), BF),
            jax.ShapeDtypeStruct((16, ROWS, D), BF),
            jax.ShapeDtypeStruct((16, ROWS, D), BF),
        ),
        in_specs=[pl.BlockSpec(memory_space=pltpu.SMEM), hbm, hbm, hbm],
        out_specs=(vmem, vmem, vmem),
        scratch_shapes=[
            pltpu.VMEM((FF, D), BF),
            pltpu.VMEM((NC, 2, 4, 96, 128), BF),
            a, a, a, a, a, a,
            pltpu.VMEM((NA, 2, 96, 128), F32),
            pltpu.VMEM((NA, 96, 128), BF),
            pltpu.VMEM((NA, 96, 128), BF),
            pltpu.VMEM((6, 4, 96, 128), BF),
            pltpu.VMEM((6, 4, 96, 128), BF),
            b, b, b, b, b, b,
            pltpu.SemaphoreType.DMA((copies,)),
            pltpu.SemaphoreType.DMA((copies,)),
            pltpu.SemaphoreType.DMA((3,)),
        ],
        compiler_params=pltpu.CompilerParams(
            collective_id=0, has_side_effects=True, vmem_limit_bytes=56 * 1024 * 1024
        ),
    )(down_mask, layer_input, out_grad, down_weight)


def grads_kernel(
    gm, um, dm, hg, gp, up, x_ref, og_ref, gw, uw,
    total, g_gate, g_up, g_down,
    xt,
):
    j = pl.program_id(0)

    @pl.when(j == 0)
    def _():
        xt[...] = x_ref[...].T
        total[...] = jnp.zeros_like(total)

    grad = jnp.concatenate([hg[0], hg[1]], axis=1).astype(F32)
    gate, upv = gp[...].astype(F32), up[...].astype(F32)
    s = jax.nn.sigmoid(gate)
    gs = gate * s
    hidden = (gs * upv).astype(BF)
    gate_grad = (grad * upv * s * (1.0 + gate * (1.0 - s))).astype(BF)
    up_grad = (grad * gs).astype(BF)

    def weight_grad(lhs, rhs, out, mask):
        acc = jnp.dot(lhs, rhs, preferred_element_type=F32)
        for a in range(acc.shape[0] // 128):
            for b in range(acc.shape[1] // 128):
                at = (slice(a * 128, a * 128 + 128), slice(b * 128, b * 128 + 128))
                out[at] = (acc[at] * mask(a, b).astype(F32)).astype(BF)

    def masked(w, mask):
        return jnp.concatenate(
            [
                jnp.concatenate(
                    [
                        w[a * 128 : a * 128 + 128, b * 128 : b * 128 + 128]
                        * mask(a, b).astype(F32).astype(BF)
                        for b in range(2)
                    ],
                    axis=1,
                )
                for a in range(D // 128)
            ],
            axis=0,
        )

    gmask = lambda a, b: gm[a, 2 * j + b]
    umask = lambda a, b: um[a, 2 * j + b]
    weight_grad(xt[...], gate_grad, g_gate, gmask)
    weight_grad(xt[...], up_grad, g_up, umask)
    weight_grad(hidden.T, og_ref[...], g_down, lambda a, b: dm[2 * j + a, b])
    nt = (((1,), (1,)), ((), ()))
    total[...] += lax.dot_general(
        gate_grad, masked(gw, gmask), nt, preferred_element_type=F32
    ) + lax.dot_general(up_grad, masked(uw, umask), nt, preferred_element_type=F32)


def grads(gate_mask, up_mask, down_mask, hg, gate_pre, up_pre, x_full, og_full, gate_weight, up_weight):
    smem = pl.BlockSpec(memory_space=pltpu.SMEM)
    cols = pl.BlockSpec((768, 256), lambda j: (0, j))
    whole = pl.BlockSpec((768, D), lambda j: (0, 0))
    weight = pl.BlockSpec((D, 256), lambda j: (0, j))
    return pl.pallas_call(
        grads_kernel,
        name="grads",
        grid=(FF // 256,),
        out_shape=(
            jax.ShapeDtypeStruct((768, D), F32),
            jax.ShapeDtypeStruct((D, FF), BF),
            jax.ShapeDtypeStruct((D, FF), BF),
            jax.ShapeDtypeStruct((FF, D), BF),
        ),
        in_specs=[
            smem, smem, smem,
            pl.BlockSpec((2, 768, 128), lambda j: (j, 0, 0)),
            cols, cols, whole, whole, weight, weight,
        ],
        out_specs=(whole, weight, weight, pl.BlockSpec((256, D), lambda j: (j, 0))),
        scratch_shapes=[pltpu.VMEM((D, 768), BF)],
        compiler_params=pltpu.CompilerParams(vmem_limit_bytes=48 * 1024 * 1024),
    )(gate_mask, up_mask, down_mask, hg, gate_pre, up_pre, x_full, og_full, gate_weight, up_weight)


def scatter_kernel(total, out, sib_out, sib_in, mine, got, send, recv):
    x, zh, zl, y, c = coords()
    sibling = device(x, zh, zl, y, 1 - c)
    peers = [
        (k, device(x, zh, lax.rem(zl + k // 4, 2), y + k % 4, c), lax.rem(zl + k // 4, 2) * 4 + lax.rem(y + k % 4, 4))
        for k in range(1, 8)
    ]
    barrier = pltpu.get_barrier_semaphore()
    for d in [sibling] + [p[1] for p in peers]:
        pl.semaphore_signal(barrier, inc=1, device_id=d, device_id_type=MESH)
    pl.semaphore_wait(barrier, 8)
    cp = Copies(send, recv)
    sib_out[...] = total[:, 1 - c].astype(BF)
    s = cp.start(0, sib_out, sib_in, sibling)
    s.wait_recv()
    mine[...] = add(total.at[:, c], sib_in).astype(BF)
    copies = [cp.start(k, mine.at[i], got.at[k], d) for k, d, i in peers]
    acc = mine[zl * 4 + y].astype(F32)
    for k, copy in zip(range(1, 8), copies):
        copy.wait_recv()
        acc = acc + got[k].astype(F32)
    out[...] = acc.astype(BF)
    cp.finish()


def scatter(total):
    vmem = pl.BlockSpec(memory_space=pltpu.VMEM)
    piece = pltpu.VMEM((8, ROWS, D), BF)
    return pl.pallas_call(
        scatter_kernel,
        name="scatter",
        out_shape=jax.ShapeDtypeStruct((ROWS, D), BF),
        in_specs=[vmem],
        out_specs=vmem,
        scratch_shapes=[
            piece, piece, piece, piece,
            pltpu.SemaphoreType.DMA((8,)),
            pltpu.SemaphoreType.DMA((8,)),
        ],
        compiler_params=pltpu.CompilerParams(
            collective_id=1, has_side_effects=True, vmem_limit_bytes=32 * 1024 * 1024
        ),
    )(total)


def shards(
    layer_input,
    out_grad,
    gate_pre,
    up_pre,
    gate_weight,
    up_weight,
    down_weight,
    gate_mask,
    up_mask,
    down_mask,
):
    hg, x_full, og_full = hidden_gradient(down_mask, layer_input, out_grad, down_weight)
    total, grad_gate, grad_up, grad_down = grads(
        gate_mask,
        up_mask,
        down_mask,
        hg.reshape(NC, 768, 128),
        gate_pre,
        up_pre,
        x_full.reshape(768, D),
        og_full.reshape(768, D),
        gate_weight,
        up_weight,
    )
    grad_input = scatter(total.reshape(8, 2, ROWS, D))
    return (grad_input, grad_gate, grad_up, grad_down)


def solution(mesh):
    in_specs = (
        P("tensor", "pipe"),
        P("tensor", "pipe"),
        P(None, "tensor"),
        P(None, "tensor"),
        P("pipe", "tensor"),
        P("pipe", "tensor"),
        P("tensor", "pipe"),
        P("pipe", "tensor"),
        P("pipe", "tensor"),
        P("tensor", "pipe"),
    )
    out_specs = (P("tensor", "pipe"), P("pipe", "tensor"), P("pipe", "tensor"), P("tensor", "pipe"))
    return jax.shard_map(shards, mesh=mesh, in_specs=in_specs, out_specs=out_specs, check_vma=False)
```

time: 405 us -> 122 us (0.30); the launches traced: 401 us -> 122 us
  waiting for transfers between devices: 299 us -> 0 us
  Pallas kernels: 0 us -> 113 us
  matrix products: 32.9 us -> 0 us
  local copies, waits for them, and re-layouts: 41.1 us -> 8.5 us
  other arithmetic: 13.7 us -> 0 us
  between operations: 14 us -> 0.71 us
    psum x1 -> x0, waiting for transfers between devices: 207 us -> none  [shards(): hidden_grad = lax.psum(hidden_partial, 'pipe')]
    pallas_call x0 -> x3, Pallas kernels: none -> 113 us  [the longest x1 74 us: hidden_gradient(): pl.pallas_call(hidden_kernel, name='hidden_gradient', out_shape=(jax.Shap...]
    all_gather x2 -> x0, waiting for transfers between devices: 52.6 us -> none  [the longest x1 37.7 us: shards(): piece = lax.all_gather(out_grad, 'tensor', axis=0, tiled=True)]
    reduce_scatter x1 -> x0, waiting for transfers between devices: 37.9 us -> none  [shards(): lax.psum_scatter(total + lax.dot_general(up_rows, up_masked, (((1,), (1,)...]
    dot_general x6 -> x0, matrix products: 32.9 us -> none  [the longest x1 7.1 us: shards(): lax.dot_general(piece, gate_rows, (((0,), (0,)), ((), ())), preferred_ele...]
    unnamed x40 -> x16, local copies, waits for them, and re-layouts: 33.3 us -> 8.5 us
    convert_element_type x5 -> x0, other arithmetic: 7.37 us -> none  [the longest x1 5.02 us: local_grads(): up_grad = (hidden_grad * gate_val * sigma_val).astype(jnp.bfloat16)]
    broadcast_in_dim x4 -> x0, local copies, waits for them, and re-layouts: 7.28 us -> none  [expand(): return jnp.repeat(jnp.repeat(mask, BLOCK, axis=0), BLOCK, axis=1)]
  transfers between devices with their start and end apart: 4 -> 0, of which waited for: 4 -> 0; matrix products, arithmetic and copies ran while one was open for 18% -> 0% of each run, Pallas kernels for 0% -> 0%
where the time goes in v1:
time: 122 us
  Pallas kernels  113 us (93%)
  local copies, waits for them, and re-layouts  8.5 us (7%)
    pallas_call x1, Pallas kernels, hidden_gradient(): pl.pallas_call(hidden_kernel, name='hidden_gradient', out_shape=(jax.Shap...  74 us
    pallas_call x1, Pallas kernels, grads(): pl.pallas_call(grads_kernel, name='grads', grid=(FF // 256,), out_shape=(...  20.7 us
    pallas_call x1, Pallas kernels, scatter(): pl.pallas_call(scatter_kernel, name='scatter', out_shape=jax.ShapeDtypeSt...  18.1 us
    unnamed x16, local copies, waits for them, and re-layouts  8.5 us

profile of v1, /device:TPU:1, one launch (start us, length us, event | category | flops | bytes accessed | tf_op | source)
XLA Modules:
  0.0 122.0 jit_solution(5886387502781894800)
XLA Ops:
  0.6 0.0 copy-start.6
  0.6 0.0 copy-start.5
  0.7 1.4 %copy.15.mask_ref.dm = s32[14,8]{1,0:T(8,128)} copy(s32[14,8]{0,1:T(8,128)} %param.19) | data formatting | bytes 896 | tf_op args[9]
  2.0 0.0 copy-start.4
  2.0 74.0 %hidden_gradient.1 = (bf16[14,2,4,96,128]{4,3,2,1,0:T(8,128)(2,1)}, bf16[16,48,1024]{2,1,0:T(8,128)(2,1)}, bf16[16,48,1024]{2,1,0:T(8,128)(2,1)}) custom-call(s32[14,8]{1,0:T(8,128)} %copy.15.mask_ref.dm, bf16[48,1024]{1,0:T(8,128)(2,1)} %x_hbm.1, bf16[48,1024]{1,0:T(8,128)(2,1)} %og_hbm.1, bf16[1792,1024]{1,0:T(8,128)(2,1)} %dw_hbm.1), custom_call_target="tpu_custom_call" | custom-call | tf_op jit(solution)/shard_map/hidden_gradient/pallas_call | solution.py:247
  76.0 0.0 copy-done.6
  76.0 0.0 copy-done.5
  76.0 0.0 copy-done.4
  76.1 0.0 copy-start.1
  76.1 1.8 %copy-done.1 = bf16[14,2,4,96,128]{4,3,2,1,0:T(8,128)(2,1)S(1)} copy-done((bf16[14,2,4,96,128]{4,3,2,1,0:T(8,128)(2,1)S(1)}, bf16[14,2,4,96,128]{4,3,2,1,0:T(8,128)(2,1)}, u32[]{:S(2)}) %copy-start.1) | copy-done | bytes 2752536
  77.8 0.0 copy-start.2
  77.8 1.4 %copy-done.2 = bf16[16,48,1024]{2,1,0:T(8,128)(2,1)S(1)} copy-done((bf16[16,48,1024]{2,1,0:T(8,128)(2,1)S(1)}, bf16[16,48,1024]{2,1,0:T(8,128)(2,1)}, u32[]{:S(2)}) %copy-start.2) | copy-done | bytes 1572888
  79.2 0.0 copy-start.3
  79.2 1.4 %copy-done.3 = bf16[16,48,1024]{2,1,0:T(8,128)(2,1)S(1)} copy-done((bf16[16,48,1024]{2,1,0:T(8,128)(2,1)S(1)}, bf16[16,48,1024]{2,1,0:T(8,128)(2,1)}, u32[]{:S(2)}) %copy-start.3) | copy-done | bytes 1572888
  80.7 20.7 %grads.1 = (f32[768,1024]{1,0:T(8,128)}, bf16[1024,1792]{1,0:T(8,128)(2,1)}, bf16[1024,1792]{1,0:T(8,128)(2,1)}, bf16[1792,1024]{1,0:T(8,128)(2,1)}) custom-call(s32[8,14]{1,0:T(8,128)S(1)} %copy-done.5, s32[8,14]{1,0:T(8,128)S(1)} %copy-done.6, s32[14,8]{1,0:T(8,128)S(1)} %copy-done.4, bf16[14,768,128]{2,1,0:T(8,128)(2,1)S(1)} %bitcast.5, ...), custom_call_target="tpu_custom_call" | custom-call | tf_op jit(solution)/shard_map/grads/pallas_call | solution.py:336
  101.3 0.0 copy-start
  101.3 1.9 %copy-done = f32[768,1024]{1,0:T(8,128)S(1)} copy-done((f32[768,1024]{1,0:T(8,128)S(1)}, f32[768,1024]{1,0:T(8,128)}, u32[]{:S(2)}) %copy-start) | copy-done | bytes 3145752
  103.2 18.1 %scatter.1 = bf16[48,1024]{1,0:T(8,128)(2,1)S(1)} custom-call(f32[8,2,48,1024]{3,2,1,0:T(8,128)S(1)} %bitcast.4), custom_call_target="tpu_custom_call" | custom-call | tf_op jit(solution)/shard_map/scatter/pallas_call | solution.py:385
  121.4 0.6 copy.17
Async XLA Ops:
  0.6 75.4 %copy-start.6 = (s32[8,14]{1,0:T(8,128)S(1)}, s32[8,14]{1,0:T(8,128)}, u32[]{:S(2)}) copy-start(s32[8,14]{1,0:T(8,128)} %um.1) | copy-start | bytes 1348
  0.6 75.4 %copy-start.5 = (s32[8,14]{1,0:T(8,128)S(1)}, s32[8,14]{1,0:T(8,128)}, u32[]{:S(2)}) copy-start(s32[8,14]{1,0:T(8,128)} %gm.1) | copy-start | bytes 1348
  2.0 74.0 %copy-start.4 = (s32[14,8]{1,0:T(8,128)S(1)}, s32[14,8]{1,0:T(8,128)}, u32[]{:S(2)}) copy-start(s32[14,8]{1,0:T(8,128)} %copy.15.mask_ref.dm) | copy-start | bytes 1348
  76.1 1.8 %copy-start.1 = (bf16[14,2,4,96,128]{4,3,2,1,0:T(8,128)(2,1)S(1)}, bf16[14,2,4,96,128]{4,3,2,1,0:T(8,128)(2,1)}, u32[]{:S(2)}) copy-start(bf16[14,2,4,96,128]{4,3,2,1,0:T(8,128)(2,1)} %get-tuple-element.11) | copy-start | bytes 8257540
  77.8 1.4 %copy-start.2 = (bf16[16,48,1024]{2,1,0:T(8,128)(2,1)S(1)}, bf16[16,48,1024]{2,1,0:T(8,128)(2,1)}, u32[]{:S(2)}) copy-start(bf16[16,48,1024]{2,1,0:T(8,128)(2,1)} %get-tuple-element.12) | copy-start | bytes 4718596
  79.2 1.4 %copy-start.3 = (bf16[16,48,1024]{2,1,0:T(8,128)(2,1)S(1)}, bf16[16,48,1024]{2,1,0:T(8,128)(2,1)}, u32[]{:S(2)}) copy-start(bf16[16,48,1024]{2,1,0:T(8,128)(2,1)} %get-tuple-element.13) | copy-start | bytes 4718596
  101.3 1.9 %copy-start = (f32[768,1024]{1,0:T(8,128)S(1)}, f32[768,1024]{1,0:T(8,128)}, u32[]{:S(2)}) copy-start(f32[768,1024]{1,0:T(8,128)} %get-tuple-element.14) | copy-start | bytes 9437188

commit v2 on v0

v2 whole, which is shorter than its diff:
```python
import jax
import jax.numpy as jnp
from jax import lax
from jax.experimental import pallas as pl
from jax.experimental.pallas import tpu as pltpu
from jax.sharding import PartitionSpec as P

MESH = pl.DeviceIdType.MESH
BF = jnp.bfloat16
F32 = jnp.float32
ROWS = 48
D = 1024
FF = 1792
NA = 8
NC = 14
GATHER = 15
VMEM = 60 * 1024 * 1024


def coords():
    p, t = lax.axis_index("pipe"), lax.axis_index("tensor")
    return (
        lax.div(p, 2),
        lax.rem(p, 2),
        lax.div(t, 8),
        lax.rem(lax.div(t, 2), 4),
        lax.rem(t, 2),
    )


def device(x, zh, zl, y, c):
    return (lax.rem(x, 4) * 2 + zh, zl * 8 + lax.rem(y, 4) * 2 + c)


def rank(zl, y, c):
    return zl * 8 + lax.rem(y, 4) * 2 + c


class Copies:
    def __init__(self, send, recv):
        self.send, self.recv, self.all = send, recv, []

    def start(self, i, src, dst, dev):
        c = pltpu.make_async_remote_copy(
            src_ref=src,
            dst_ref=dst,
            send_sem=self.send.at[i],
            recv_sem=self.recv.at[i],
            device_id=dev,
            device_id_type=MESH,
        )
        c.start()
        self.all.append(c)
        return c

    def finish(self):
        for c in self.all:
            c.wait_send()


class Gather:
    def __init__(self, cp, base, src, full, sem):
        self.cp, self.base, self.full, self.src = cp, base, full, src
        x, zh, zl, y, c = self.at = coords()
        self.me = full.at[rank(zl, y, c)]
        self.own = pltpu.make_async_copy(src, self.me, sem)
        self.own.start()
        self.z = cp.start(base, src, self.me, device(x, zh, 1 - zl, y, c))
        self.n = 7

    def start_y(self):
        x, zh, zl, y, c = self.at
        self.y1 = [
            self.cp.start(self.base + k, self.src, self.me, device(x, zh, zl, y + k, c)) for k in (1, 3, 2)
        ]
        self.sib = [self.cp.start(self.base + 7, self.src, self.me, device(x, zh, zl, y, 1 - c))]

    def to_sibling(self, r):
        x, zh, zl, y, c = self.at
        self.n += 1
        piece = self.full.at[r]
        self.sib.append(self.cp.start(self.base + self.n, piece, piece, device(x, zh, zl, y, 1 - c)))

    def step_z(self):
        x, zh, zl, y, c = self.at
        self.z.wait_recv()
        piece = self.full.at[rank(1 - zl, y, c)]
        self.y2 = [
            self.cp.start(self.base + 3 + k, piece, piece, device(x, zh, zl, y + k, c)) for k in (1, 3, 2)
        ]
        self.to_sibling(rank(1 - zl, y, c))

    def step_y(self):
        x, zh, zl, y, c = self.at
        for copies, z in ((self.y1, zl), (self.y2, 1 - zl)):
            for copy, k in zip(copies, (1, 3, 2)):
                copy.wait_recv()
                self.to_sibling(rank(z, y + 4 - k, c))

    def finish(self):
        for copy in self.sib:
            copy.wait_recv()
        self.own.wait()


def add(*refs):
    total = refs[0][...].astype(F32)
    for r in refs[1:]:
        total = total + r[...].astype(F32)
    return total


def mask_columns(w, mask_ref):
    @pl.loop(0, NC)
    def _(j):
        for k in range(D // 128):
            at = (pl.ds(k * 128, 128), pl.ds(pl.multiple_of(j * 128, 128), 128))
            w[at] = w[at] * mask_ref[k, j].astype(F32).astype(BF)


NT = (((1,), (1,)), ((), ()))


def main_kernel(
    dm, gm, um, x_hbm, og_hbm, gp_hbm, up_hbm, gw_hbm, uw_hbm, dw_hbm,
    gg_out, ug_out, xt_out, gd_out, out,
    x_full, og_full, dw, gp, up, gw, uw,
    hf, hb, hg, gg, ug, total, xt,
    rl1, rl2, rl3, rr1, rr2, rr3, asum, fa, rz,
    rb, bf, bs, bl1, bl2, bl3, br1, br2, br3,
    sib_in, mine, got, out_f,
    send, recv, local,
):
    x, zh, zl, y, c = coords()
    right, left = device(x + 1, zh, zl, y, c), device(x + 3, zh, zl, y, c)
    other, sibling = device(x, 1 - zh, zl, y, c), device(x, zh, zl, y, 1 - c)
    x1, x2, x3 = lax.rem(x + 1, 4), lax.rem(x + 2, 4), lax.rem(x + 3, 4)

    loads = [
        pltpu.make_async_copy(src, dst, local.at[i])
        for i, (src, dst) in enumerate(
            ((dw_hbm, dw), (gp_hbm, gp), (up_hbm, up), (gw_hbm, gw), (uw_hbm, uw))
        )
    ]
    for load in loads:
        load.start()
    zl_peer = [device(x, zh, 1 - zl, y + k, c) for k in range(4)]
    y_peer = [device(x, zh, zl, y + k, c) for k in (1, 2, 3)]
    partners = [right, left, other, sibling] + zl_peer + y_peer
    barrier = pltpu.get_barrier_semaphore()
    for d in partners:
        pl.semaphore_signal(barrier, inc=1, device_id=d, device_id_type=MESH)
    pl.semaphore_wait(barrier, len(partners))

    cp = Copies(send, recv)
    og = Gather(cp, 0, og_hbm, og_full, local.at[5])
    og.start_y()
    inp = Gather(cp, GATHER, x_hbm, x_full, local.at[6])
    loads[0].wait()

    @pl.loop(0, NC)
    def _(i):
        for k in range(D // 128):
            at = (pl.ds(pl.multiple_of(i * 128, 128), 128), pl.ds(k * 128, 128))
            dw[at] = dw[at] * dm[k, i].astype(F32).astype(BF)

    og.step_z()
    inp.start_y()
    og.step_y()
    og.finish()

    def partial(first, last, step):
        @pl.loop(first, last, step=step)
        def _(j):
            w = dw[pl.ds(pl.multiple_of(j * 256, 256), 256), :]
            acc = lax.dot_general(og_full[...].reshape(768, D), w, NT, preferred_element_type=F32)
            for b in range(2):
                v = acc[:, b * 128 : b * 128 + 128].reshape(2, 4, 96, 128)
                hf[2 * j + b] = v
                hb[2 * j + b] = v.astype(BF)

    B = pl.ds(NA, 6)
    BL, BR = pl.ds(0, 3), pl.ds(3, 3)
    HBL, HBR = pl.ds(NA, 3), pl.ds(NA + 3, 3)
    GA = (pl.ds(0, 2), pl.ds(2, 2))
    AL, AR = GA, (pl.ds(4, 2), pl.ds(6, 2))
    s = 2 * GATHER
    partial(4, 7, 1)
    zb = [
        cp.start(s + i, hb.at[B, 1 - zh, q], rb.at[:, q], other) for i, q in enumerate((x2, x1, x3, x))
    ]
    a1, a2 = [], []
    for g in range(2):
        partial(g, g + 3, 2)
        i = s + 4 + 6 * g
        a1.append(
            (
                cp.start(i, hb.at[AL[g], :, x2], rl1.at[GA[g]], right),
                cp.start(i + 1, hb.at[AR[g], :, x2], rr1.at[GA[g]], left),
            )
        )
        a2.append(
            (
                cp.start(i + 2, hb.at[AR[g], :, x1], rl2.at[GA[g]], right),
                cp.start(i + 3, hb.at[AL[g], :, x3], rr2.at[GA[g]], left),
            )
        )
    inp.step_z()
    loads[1].wait()
    loads[2].wait()

    def down(first, last):
        @pl.loop(first, last)
        def _(j):
            rows = pl.ds(pl.multiple_of(j * 256, 256), 256)
            gate, upv = gp[:, rows].astype(F32), up[:, rows].astype(F32)
            hidden = (gate * jax.nn.sigmoid(gate) * upv).astype(BF)
            dw[rows, :] = jnp.dot(
                hidden.T, og_full[...].reshape(768, D), preferred_element_type=F32
            ).astype(BF)

    a3 = []

    def turn_a(g):
        a1[g][0].wait_recv()
        rl1[GA[g]] = add(rl1.at[GA[g]], hf.at[AL[g], :, x1]).astype(BF)
        r = cp.start(s + 8 + 6 * g, rl1.at[GA[g]], rl3.at[GA[g]], right)
        a1[g][1].wait_recv()
        rr1[GA[g]] = add(rr1.at[GA[g]], hf.at[AR[g], :, x3]).astype(BF)
        a3.append((r, cp.start(s + 9 + 6 * g, rr1.at[GA[g]], rr3.at[GA[g]], left)))

    def land_b(i, q):
        zb[i].wait_recv()
        v = add(rb.at[:, q], hf.at[B, zh, q])
        bf[:, q] = v
        bs[:, q] = v.astype(BF)

    za = []

    def land_a(g):
        for copy in a2[g] + a3[g]:
            copy.wait_recv()
        asum[AL[g]] = add(hf.at[AL[g], :, x], rl3.at[GA[g]], rr2.at[GA[g]])
        asum[AR[g]] = add(hf.at[AR[g], :, x], rr3.at[GA[g]], rl2.at[GA[g]])
        for k, cols in enumerate((AL[g], AR[g])):
            fa[cols] = asum[cols, 1 - zh].astype(BF)
            za.append(cp.start(s + 16 + 2 * g + k, fa.at[cols], rz.at[cols], other))

    down(0, 2)
    turn_a(0)
    land_b(0, x2)
    b1r = cp.start(s + 20, bs.at[BL, x2], bl1, right)
    b1l = cp.start(s + 21, bs.at[BR, x2], br1, left)
    down(2, 3)
    turn_a(1)
    land_b(1, x1)
    b2r = cp.start(s + 22, bs.at[BR, x1], bl2, right)
    b1r.wait_recv()
    bl1[...] = add(bl1, bf.at[BL, x1]).astype(BF)
    b3r = cp.start(s + 23, bl1, bl3, right)
    down(3, 5)
    land_b(2, x3)
    b2l = cp.start(s + 24, bs.at[BL, x3], br2, left)
    b1l.wait_recv()
    br1[...] = add(br1, bf.at[BR, x3]).astype(BF)
    b3l = cp.start(s + 25, br1, br3, left)
    inp.step_y()
    land_a(0)
    land_b(3, x)
    land_a(1)
    down(5, 7)
    gd = pltpu.make_async_copy(dw, gd_out, local.at[0])
    gd.start()

    g = s + 26
    A, FL, FR = pl.ds(0, NA), pl.ds(0, 4), pl.ds(4, 4)

    def send_rows(i, cols, h, q, dev):
        piece = hg.at[cols, h, q]
        return cp.start(g + i, piece, piece, dev)

    for copy in (b2r, b2l, b3r, b3l):
        copy.wait_recv()
    hg[HBL, zh, x] = add(bf.at[BL, x], bl3, br2).astype(BF)
    hg[HBR, zh, x] = add(bf.at[BR, x], br3, bl2).astype(BF)
    br = send_rows(0, B, zh, x, right)
    bl = send_rows(1, B, zh, x, left)
    z = [send_rows(2, B, zh, x, other)]
    for copy in za:
        copy.wait_recv()
    hg[A, zh, x] = add(asum.at[:, zh], rz).astype(BF)
    ga = send_rows(3, A, zh, x, other)
    gr = [send_rows(4, A, zh, x, right)]
    gl = [send_rows(5, A, zh, x, left)]
    inp.finish()
    xt[...] = x_full[...].reshape(768, D).T
    xt_copy = pltpu.make_async_copy(xt, xt_out, local.at[5])
    xt_copy.start()
    loads[3].wait()
    mask_columns(gw, gm)
    br.wait_recv()
    fr = send_rows(6, HBL, zh, x3, right)
    z.append(send_rows(7, B, zh, x3, other))
    bl.wait_recv()
    fl = send_rows(8, HBR, zh, x1, left)
    z.append(send_rows(9, B, zh, x1, other))
    loads[4].wait()
    mask_columns(uw, um)
    gr[0].wait_recv()
    f0 = [send_rows(10, FL, zh, x3, right)]
    gl[0].wait_recv()
    f0.append(send_rows(11, FR, zh, x1, left))
    ga.wait_recv()
    gr.append(send_rows(12, A, 1 - zh, x, right))
    gl.append(send_rows(13, A, 1 - zh, x, left))
    fr.wait_recv()
    z.append(send_rows(14, HBL, zh, x2, other))
    fl.wait_recv()
    z.append(send_rows(15, HBR, zh, x2, other))

    def local_grads(h, first, last):
        rows = pl.ds(pl.multiple_of(h * 384, 128), 384)

        @pl.loop(first // 2, last // 2)
        def _(j):
            cols = pl.ds(pl.multiple_of(j * 256, 256), 256)
            gate, upv = gp[rows, cols].astype(F32), up[rows, cols].astype(F32)
            grad = jnp.concatenate(
                [hg[2 * j + b, h].reshape(384, 128).astype(F32) for b in range(2)], axis=1
            )
            sig = jax.nn.sigmoid(gate)
            gate_grad = (grad * upv * sig * (1.0 + gate * (1.0 - sig))).astype(BF)
            up_grad = (grad * gate * sig).astype(BF)
            for b in range(2):
                at = slice(b * 128, b * 128 + 128)
                gg[2 * j + b, h] = gate_grad[:, at].reshape(4, 96, 128)
                ug[2 * j + b, h] = up_grad[:, at].reshape(4, 96, 128)
            v = lax.dot_general(gate_grad, gw[:, cols], NT, preferred_element_type=F32)
            v = v + lax.dot_general(up_grad, uw[:, cols], NT, preferred_element_type=F32)
            total[h] += v.reshape(4, 2, ROWS, D)

    def write(h, i):
        copies = [
            pltpu.make_async_copy(gg.at[:, h], gg_out.at[:, h], local.at[1 + i]),
            pltpu.make_async_copy(ug.at[:, h], ug_out.at[:, h], local.at[2 + i]),
        ]
        for copy in copies:
            copy.start()
        return copies

    r = g + 18

    def to_sibling(h, i):
        return cp.start(g + 16 + i, total.at[h, :, 1 - c], sib_in.at[i], sibling)

    def piece(h, k, near, q):
        n = 4 * near + k
        return pltpu.make_async_remote_copy(
            src_ref=mine.at[h, q],
            dst_ref=got.at[n],
            send_sem=send.at[r + n],
            recv_sem=recv.at[r + n],
            device_id=device(x, zh, h, y + k, c),
            device_id_type=MESH,
        )

    def spread(h, i, copy):
        copy.wait_recv()
        mine[h] = (total[h, :, c] + sib_in[i]).astype(BF)
        near = lax.rem(h + zl, 2)

        @pl.when(near == 1)
        def _():
            piece(h, 0, near, y).start()

        for k in (1, 3, 2):
            piece(h, k, near, lax.rem(y + k, 4)).start()

    total[...] = jnp.zeros_like(total)
    local_grads(zh, 8, 14)
    for copy in f0:
        copy.wait_recv()
    local_grads(zh, 0, 8)
    near = to_sibling(zh, 0)
    writes = write(zh, 0)
    gr[1].wait_recv()
    f1 = [send_rows(18 + 8, FL, 1 - zh, x3, right)]
    gl[1].wait_recv()
    f1.append(send_rows(18 + 9, FR, 1 - zh, x1, left))
    spread(zh, 0, near)
    for copy in f1 + z:
        copy.wait_recv()
    local_grads(1 - zh, 0, 14)
    spread(1 - zh, 1, to_sibling(1 - zh, 1))
    writes += write(1 - zh, 2)
    out_f[...] = total[zl, y, c] + sib_in[lax.rem(zl + zh, 2), y]
    for n in range(1, 8):
        wait = piece(lax.rem(zl + n // 4, 2), n % 4, n // 4, y)
        wait.wait_recv()
        wait.wait_send()
        out_f[...] += got[n].astype(F32)
    out[...] = out_f[...].astype(BF)
    for copy in writes + [gd, xt_copy]:
        copy.wait()
    cp.finish()


def main(dm, gm, um, layer_input, out_grad, gate_pre, up_pre, gate_weight, up_weight, down_weight):
    vmem = pl.BlockSpec(memory_space=pltpu.VMEM)
    hbm = pl.BlockSpec(memory_space=pl.ANY)
    smem = pl.BlockSpec(memory_space=pltpu.SMEM)
    blocks = (NC, 2, 4, 96, 128)
    a = pltpu.VMEM((4, 2, 96, 128), BF)
    b = pltpu.VMEM((3, 96, 128), BF)
    copies = 2 * GATHER + 26 + 18 + 8 + 2
    return pl.pallas_call(
        main_kernel,
        name="main",
        out_shape=(
            jax.ShapeDtypeStruct(blocks, BF),
            jax.ShapeDtypeStruct(blocks, BF),
            jax.ShapeDtypeStruct((D, 768), BF),
            jax.ShapeDtypeStruct((FF, D), BF),
            jax.ShapeDtypeStruct((ROWS, D), BF),
        ),
        in_specs=[smem] * 3 + [hbm] * 7,
        out_specs=(hbm, hbm, hbm, hbm, vmem),
        scratch_shapes=[
            pltpu.VMEM((16, ROWS, D), BF),
            pltpu.VMEM((16, ROWS, D), BF),
            pltpu.VMEM((FF, D), BF),
            pltpu.VMEM((768, FF), BF),
            pltpu.VMEM((768, FF), BF),
            pltpu.VMEM((D, FF), BF),
            pltpu.VMEM((D, FF), BF),
            pltpu.VMEM(blocks, F32),
            pltpu.VMEM(blocks, BF),
            pltpu.VMEM(blocks, BF),
            pltpu.VMEM(blocks, BF),
            pltpu.VMEM(blocks, BF),
            pltpu.VMEM((2, 4, 2, ROWS, D), F32),
            pltpu.VMEM((D, 768), BF),
            a, a, a, a, a, a,
            pltpu.VMEM((NA, 2, 96, 128), F32),
            pltpu.VMEM((NA, 96, 128), BF),
            pltpu.VMEM((NA, 96, 128), BF),
            pltpu.VMEM((6, 4, 96, 128), BF),
            pltpu.VMEM((6, 4, 96, 128), F32),
            pltpu.VMEM((6, 4, 96, 128), BF),
            b, b, b, b, b, b,
            pltpu.VMEM((2, 4, ROWS, D), F32),
            pltpu.VMEM((2, 4, ROWS, D), BF),
            pltpu.VMEM((8, ROWS, D), BF),
            pltpu.VMEM((ROWS, D), F32),
            pltpu.SemaphoreType.DMA((copies,)),
            pltpu.SemaphoreType.DMA((copies,)),
            pltpu.SemaphoreType.DMA((7,)),
        ],
        compiler_params=pltpu.CompilerParams(
            collective_id=0, has_side_effects=True, vmem_limit_bytes=VMEM
        ),
    )(dm, gm, um, layer_input, out_grad, gate_pre, up_pre, gate_weight, up_weight, down_weight)


def weights_kernel(dm, gm, um, gg, ug, xt, gd, g_gate, g_up, g_down):
    j = pl.program_id(0)
    for grad, out, mask in ((gg, g_gate, gm), (ug, g_up, um)):
        rhs = jnp.concatenate([grad[0], grad[1]], axis=1)
        acc = jnp.dot(xt[...], rhs, preferred_element_type=F32)
        for a in range(D // 128):
            for b in range(2):
                at = (slice(a * 128, a * 128 + 128), slice(b * 128, b * 128 + 128))
                out[at] = (acc[at] * mask[a, 2 * j + b].astype(F32)).astype(BF)
    for a in range(2):
        for b in range(D // 128):
            at = (slice(a * 128, a * 128 + 128), slice(b * 128, b * 128 + 128))
            g_down[at] = gd[at] * dm[b, 2 * j + a].astype(F32).astype(BF)


def weights(dm, gm, um, gg, ug, xt, gd):
    smem = pl.BlockSpec(memory_space=pltpu.SMEM)
    cols = pl.BlockSpec((2, 768, 128), lambda j: (j, 0, 0))
    weight = pl.BlockSpec((D, 256), lambda j: (0, j))
    down = pl.BlockSpec((256, D), lambda j: (j, 0))
    return pl.pallas_call(
        weights_kernel,
        name="weights",
        grid=(FF // 256,),
        out_shape=(
            jax.ShapeDtypeStruct((D, FF), BF),
            jax.ShapeDtypeStruct((D, FF), BF),
            jax.ShapeDtypeStruct((FF, D), BF),
        ),
        in_specs=[smem, smem, smem, cols, cols, pl.BlockSpec((D, 768), lambda j: (0, 0)), down],
        out_specs=(weight, weight, down),
        compiler_params=pltpu.CompilerParams(vmem_limit_bytes=VMEM),
    )(dm, gm, um, gg, ug, xt, gd)


def shards(
    layer_input,
    out_grad,
    gate_pre,
    up_pre,
    gate_weight,
    up_weight,
    down_weight,
    gate_mask,
    up_mask,
    down_mask,
):
    masks = (down_mask.T, gate_mask, up_mask)
    gg, ug, xt, gd, grad_input = main(
        *masks, layer_input, out_grad, gate_pre, up_pre, gate_weight, up_weight, down_weight
    )
    grad_gate, grad_up, grad_down = weights(
        *masks, gg.reshape(NC, 768, 128), ug.reshape(NC, 768, 128), xt, gd
    )
    return (grad_input, grad_gate, grad_up, grad_down)


def solution(mesh):
    in_specs = (
        P("tensor", "pipe"),
        P("tensor", "pipe"),
        P(None, "tensor"),
        P(None, "tensor"),
        P("pipe", "tensor"),
        P("pipe", "tensor"),
        P("tensor", "pipe"),
        P("pipe", "tensor"),
        P("pipe", "tensor"),
        P("tensor", "pipe"),
    )
    out_specs = (P("tensor", "pipe"), P("pipe", "tensor"), P("pipe", "tensor"), P("tensor", "pipe"))
    return jax.shard_map(shards, mesh=mesh, in_specs=in_specs, out_specs=out_specs, check_vma=False)
```

time: 405 us -> 99.9 us (0.25)
  waiting for transfers between devices: 299 us -> 0 us
  Pallas kernels: 0 us -> 98.2 us
  local copies, waits for them, and re-layouts: 41.1 us -> 0.64 us
  matrix products: 32.9 us -> 0 us
  other arithmetic: 13.7 us -> 0 us
  between operations: 14 us -> 0.65 us
    psum x1 -> x0, waiting for transfers between devices: 207 us -> none  [shards(): hidden_grad = lax.psum(hidden_partial, 'pipe')]
    pallas_call x0 -> x2, Pallas kernels: none -> 98.2 us  [the longest x1 85.2 us: main(): pl.pallas_call(main_kernel, name='main', out_shape=(jax.ShapeDtypeStruct(...]
    all_gather x2 -> x0, waiting for transfers between devices: 52.6 us -> none  [the longest x1 37.7 us: shards(): piece = lax.all_gather(out_grad, 'tensor', axis=0, tiled=True)]
    reduce_scatter x1 -> x0, waiting for transfers between devices: 37.9 us -> none  [shards(): lax.psum_scatter(total + lax.dot_general(up_rows, up_masked, (((1,), (1,)...]
    dot_general x6 -> x0, matrix products: 32.9 us -> none  [the longest x1 7.1 us: shards(): lax.dot_general(piece, gate_rows, (((0,), (0,)), ((), ())), preferred_ele...]
    unnamed x40 -> x3, local copies, waits for them, and re-layouts: 33.3 us -> 0.64 us
    convert_element_type x5 -> x0, other arithmetic: 7.37 us -> none  [the longest x1 5.02 us: local_grads(): up_grad = (hidden_grad * gate_val * sigma_val).astype(jnp.bfloat16)]
    broadcast_in_dim x4 -> x0, local copies, waits for them, and re-layouts: 7.28 us -> none  [expand(): return jnp.repeat(jnp.repeat(mask, BLOCK, axis=0), BLOCK, axis=1)]
  transfers between devices with their start and end apart: 4 -> 0, of which waited for: 4 -> 0; matrix products, arithmetic and copies ran while one was open for 18% -> 0% of each run, Pallas kernels for 0% -> 0%
where the time goes in v2:
time: 99.9 us; the launch traced here: 99.5 us
  Pallas kernels  98.2 us (98%)
    pallas_call x1, Pallas kernels, main(): pl.pallas_call(main_kernel, name='main', out_shape=(jax.ShapeDtypeStruct(...  85.2 us
    pallas_call x1, Pallas kernels, weights(): pl.pallas_call(weights_kernel, name='weights', grid=(FF // 256,), out_sha...  13 us

profile of v2, /device:TPU:1, one launch (start us, length us, event | category | flops | bytes accessed | tf_op | source)
XLA Modules:
  0.0 99.5 jit_solution(2006355364567290049)
XLA Ops:
  0.6 85.2 %main.1 = (bf16[14,2,4,96,128]{4,3,2,1,0:T(8,128)(2,1)}, bf16[14,2,4,96,128]{4,3,2,1,0:T(8,128)(2,1)}, bf16[1024,768]{1,0:T(8,128)(2,1)}, bf16[1792,1024]{1,0:T(8,128)(2,1)}, bf16[48,1024]{1,0:T(8,128)(2,1)}) custom-call(s32[8,14]{1,0:T(8,128)} %bitcast.5, s32[8,14]{1,0:T(8,128)} %gm.3, s32[8,14]{1,0:T(8,128)} %um.3, bf16[48,1024]{1,0:T(8,128)(2,1)} %x_hbm.1, ...), custom_call_target="tpu_custom_call" | custom-call | tf_op jit(solution)/shard_map/main/pallas_call | solution.py:416
  85.8 0.0 copy-start
  85.9 13.0 %weights.1 = (bf16[1024,1792]{1,0:T(8,128)(2,1)}, bf16[1024,1792]{1,0:T(8,128)(2,1)}, bf16[1792,1024]{1,0:T(8,128)(2,1)}) custom-call(s32[8,14]{1,0:T(8,128)} %bitcast.6, s32[8,14]{1,0:T(8,128)} %gm.3, s32[8,14]{1,0:T(8,128)} %um.3, bf16[14,768,128]{2,1,0:T(8,128)(2,1)} %bitcast.3, bf16[14,768,128]{2,1,0:T(8,128)(2,1)} %bitcast.4, ...), custom_call_target="tpu_custom_call" | custom-call | tf_op jit(solution)/shard_map/weights/pallas_call | solution.py:485
  98.9 0.0 copy-done
  98.9 0.6 copy.15
Async XLA Ops:
  85.8 13.0 %copy-start = (bf16[48,1024]{1,0:T(8,128)(2,1)S(1)}, bf16[48,1024]{1,0:T(8,128)(2,1)}, u32[]{:S(2)}) copy-start(bf16[48,1024]{1,0:T(8,128)(2,1)} %get-tuple-element.24) | copy-start | bytes 294916

commit v3 on v2

--- a/solution.py
+++ b/solution.py
@@ -14,7 +14,9 @@
 NA = 8
 NC = 14
 GATHER = 15
-VMEM = 60 * 1024 * 1024
+VMEM = 63 * 1024 * 1024
+PARTS = 4
+COLS = D // PARTS
 
 
 def coords():
@@ -32,8 +34,9 @@
     return (lax.rem(x, 4) * 2 + zh, zl * 8 + lax.rem(y, 4) * 2 + c)
 
 
-def rank(zl, y, c):
-    return zl * 8 + lax.rem(y, 4) * 2 + c
+def place(zl, y, c):
+    y = lax.rem(y, 4)
+    return lax.rem(y, 2) * 8 + zl * 4 + lax.div(y, 2) * 2 + c
 
 
 class Copies:
@@ -59,21 +62,16 @@
 
 
 class Gather:
-    def __init__(self, cp, base, src, full, sem):
-        self.cp, self.base, self.full, self.src = cp, base, full, src
+    def __init__(self, cp, base, src, full, own):
+        self.cp, self.base, self.full, self.src, self.own = cp, base, full, src, own
         x, zh, zl, y, c = self.at = coords()
-        self.me = full.at[rank(zl, y, c)]
-        self.own = pltpu.make_async_copy(src, self.me, sem)
-        self.own.start()
+        self.me = full.at[place(zl, y, c)]
         self.z = cp.start(base, src, self.me, device(x, zh, 1 - zl, y, c))
         self.n = 7
-
-    def start_y(self):
-        x, zh, zl, y, c = self.at
         self.y1 = [
-            self.cp.start(self.base + k, self.src, self.me, device(x, zh, zl, y + k, c)) for k in (1, 3, 2)
+            cp.start(base + k, src, self.me, device(x, zh, zl, y + k, c)) for k in (1, 3, 2)
         ]
-        self.sib = [self.cp.start(self.base + 7, self.src, self.me, device(x, zh, zl, y, 1 - c))]
+        self.sib = [cp.start(base + 7, src, self.me, device(x, zh, zl, y, 1 - c))]
 
     def to_sibling(self, r):
         x, zh, zl, y, c = self.at
@@ -84,23 +82,29 @@
     def step_z(self):
         x, zh, zl, y, c = self.at
         self.z.wait_recv()
-        piece = self.full.at[rank(1 - zl, y, c)]
+        piece = self.full.at[place(1 - zl, y, c)]
         self.y2 = [
             self.cp.start(self.base + 3 + k, piece, piece, device(x, zh, zl, y + k, c)) for k in (1, 3, 2)
         ]
-        self.to_sibling(rank(1 - zl, y, c))
-
-    def step_y(self):
+        self.to_sibling(place(1 - zl, y, c))
+
+    def step_y(self, copies, z):
         x, zh, zl, y, c = self.at
-        for copies, z in ((self.y1, zl), (self.y2, 1 - zl)):
-            for copy, k in zip(copies, (1, 3, 2)):
-                copy.wait_recv()
-                self.to_sibling(rank(z, y + 4 - k, c))
-
-    def finish(self):
+        for copy, k in zip(copies, (1, 3, 2)):
+            copy.wait_recv()
+            self.to_sibling(place(z, y + 4 - k, c))
+
+    def near(self):
+        self.step_y(self.y1, self.at[2])
+        for copy in [self.sib[0]] + self.sib[2:]:
+            copy.wait_recv()
+        self.own.wait()
+        self.sib = [self.sib[1]]
+
+    def far(self):
+        self.step_y(self.y2, 1 - self.at[2])
         for copy in self.sib:
             copy.wait_recv()
-        self.own.wait()
 
 
 def add(*refs):
@@ -125,10 +129,10 @@
     dm, gm, um, x_hbm, og_hbm, gp_hbm, up_hbm, gw_hbm, uw_hbm, dw_hbm,
     gg_out, ug_out, xt_out, gd_out, out,
     x_full, og_full, dw, gp, up, gw, uw,
-    hf, hb, hg, gg, ug, total, xt,
+    hf, hb, hg, gg, ug, by_gate, by_up, total, xt,
     rl1, rl2, rl3, rr1, rr2, rr3, asum, fa, rz,
     rb, bf, bs, bl1, bl2, bl3, br1, br2, br3,
-    sib_in, mine, got, out_f,
+    sib_in, mine, got,
     send, recv, local,
 ):
     x, zh, zl, y, c = coords()
@@ -136,14 +140,13 @@
     other, sibling = device(x, 1 - zh, zl, y, c), device(x, zh, zl, y, 1 - c)
     x1, x2, x3 = lax.rem(x + 1, 4), lax.rem(x + 2, 4), lax.rem(x + 3, 4)
 
-    loads = [
-        pltpu.make_async_copy(src, dst, local.at[i])
-        for i, (src, dst) in enumerate(
-            ((dw_hbm, dw), (gp_hbm, gp), (up_hbm, up), (gw_hbm, gw), (uw_hbm, uw))
-        )
-    ]
-    for load in loads:
-        load.start()
+    load_dw = pltpu.make_async_copy(dw_hbm, dw, local.at[0])
+    load_dw.start()
+    here = place(zl, y, c)
+    own_og = pltpu.make_async_copy(og_hbm, og_full.at[here], local.at[1])
+    own_og.start()
+    own_x = pltpu.make_async_copy(x_hbm, x_full.at[here], local.at[2])
+    own_x.start()
     zl_peer = [device(x, zh, 1 - zl, y + k, c) for k in range(4)]
     y_peer = [device(x, zh, zl, y + k, c) for k in (1, 2, 3)]
     partners = [right, left, other, sibling] + zl_peer + y_peer
@@ -153,10 +156,8 @@
     pl.semaphore_wait(barrier, len(partners))
 
     cp = Copies(send, recv)
-    og = Gather(cp, 0, og_hbm, og_full, local.at[5])
-    og.start_y()
-    inp = Gather(cp, GATHER, x_hbm, x_full, local.at[6])
-    loads[0].wait()
+    og = Gather(cp, 0, og_hbm, og_full, own_og)
+    load_dw.wait()
 
     @pl.loop(0, NC)
     def _(i):
@@ -165,19 +166,30 @@
             dw[at] = dw[at] * dm[k, i].astype(F32).astype(BF)
 
     og.step_z()
-    inp.start_y()
-    og.step_y()
-    og.finish()
-
-    def partial(first, last, step):
+    inp = Gather(cp, GATHER, x_hbm, x_full, own_x)
+    loads = []
+    for i, (src, dst) in enumerate(((gp_hbm, gp), (up_hbm, up))):
+        for h in range(2):
+            loads.append(pltpu.make_async_copy(src.at[:, :, h], dst.at[h], local.at[3 + 2 * i + h]))
+    for load in loads:
+        load.start()
+
+    def partial(z, first, last, step):
         @pl.loop(first, last, step=step)
         def _(j):
             w = dw[pl.ds(pl.multiple_of(j * 256, 256), 256), :]
-            acc = lax.dot_general(og_full[...].reshape(768, D), w, NT, preferred_element_type=F32)
+            rows = [og_full[pl.ds(8 * h + 4 * z, 4)].reshape(192, D) for h in range(2)]
+            acc = lax.dot_general(
+                jnp.concatenate(rows, axis=0), w, NT, preferred_element_type=F32
+            )
             for b in range(2):
-                v = acc[:, b * 128 : b * 128 + 128].reshape(2, 4, 96, 128)
-                hf[2 * j + b] = v
-                hb[2 * j + b] = v.astype(BF)
+                v = acc[:, b * 128 : b * 128 + 128].reshape(2, 2, 96, 128)
+                hf[2 * j + b, :, pl.ds(2 * z, 2)] = v
+                hb[2 * j + b, :, pl.ds(2 * z, 2)] = v.astype(BF)
+
+    og.near()
+    partial(zl, 0, 7, 1)
+    og.far()
 
     B = pl.ds(NA, 6)
     BL, BR = pl.ds(0, 3), pl.ds(3, 3)
@@ -185,13 +197,13 @@
     GA = (pl.ds(0, 2), pl.ds(2, 2))
     AL, AR = GA, (pl.ds(4, 2), pl.ds(6, 2))
     s = 2 * GATHER
-    partial(4, 7, 1)
+    partial(1 - zl, 4, 7, 1)
     zb = [
         cp.start(s + i, hb.at[B, 1 - zh, q], rb.at[:, q], other) for i, q in enumerate((x2, x1, x3, x))
     ]
     a1, a2 = [], []
     for g in range(2):
-        partial(g, g + 3, 2)
+        partial(1 - zl, g, g + 3, 2)
         i = s + 4 + 6 * g
         a1.append(
             (
@@ -206,15 +218,27 @@
             )
         )
     inp.step_z()
-    loads[1].wait()
-    loads[2].wait()
+    for load in loads:
+        load.wait()
+    load_gw = pltpu.make_async_copy(gw_hbm, gw, local.at[0])
+    load_gw.start()
+    load_uw = pltpu.make_async_copy(uw_hbm, uw, local.at[1])
+    load_uw.start()
 
     def down(first, last):
         @pl.loop(first, last)
         def _(j):
             rows = pl.ds(pl.multiple_of(j * 256, 256), 256)
-            gate, upv = gp[:, rows].astype(F32), up[:, rows].astype(F32)
-            hidden = (gate * jax.nn.sigmoid(gate) * upv).astype(BF)
+            gate = gp[..., rows].reshape(768, 256).astype(F32)
+            upv = up[..., rows].reshape(768, 256).astype(F32)
+            sig = jax.nn.sigmoid(gate)
+            gated = gate * sig
+            hidden = (gated * upv).astype(BF)
+            factor = upv * sig * (1.0 + gate * (1.0 - sig))
+            for b in range(2):
+                at = slice(b * 128, b * 128 + 128)
+                by_gate[2 * j + b] = factor[:, at].reshape(2, 4, 96, 128)
+                by_up[2 * j + b] = gated[:, at].reshape(2, 4, 96, 128)
             dw[rows, :] = jnp.dot(
                 hidden.T, og_full[...].reshape(768, D), preferred_element_type=F32
             ).astype(BF)
@@ -264,12 +288,12 @@
     b1l.wait_recv()
     br1[...] = add(br1, bf.at[BR, x3]).astype(BF)
     b3l = cp.start(s + 25, br1, br3, left)
-    inp.step_y()
+    inp.near()
     land_a(0)
     land_b(3, x)
     land_a(1)
     down(5, 7)
-    gd = pltpu.make_async_copy(dw, gd_out, local.at[0])
+    gd = pltpu.make_async_copy(dw, gd_out, local.at[3])
     gd.start()
 
     g = s + 26
@@ -292,11 +316,11 @@
     ga = send_rows(3, A, zh, x, other)
     gr = [send_rows(4, A, zh, x, right)]
     gl = [send_rows(5, A, zh, x, left)]
-    inp.finish()
+    inp.far()
     xt[...] = x_full[...].reshape(768, D).T
-    xt_copy = pltpu.make_async_copy(xt, xt_out, local.at[5])
+    xt_copy = pltpu.make_async_copy(xt, xt_out, local.at[4])
     xt_copy.start()
-    loads[3].wait()
+    load_gw.wait()
     mask_columns(gw, gm)
     br.wait_recv()
     fr = send_rows(6, HBL, zh, x3, right)
@@ -304,7 +328,7 @@
     bl.wait_recv()
     fl = send_rows(8, HBR, zh, x1, left)
     z.append(send_rows(9, B, zh, x1, other))
-    loads[4].wait()
+    load_uw.wait()
     mask_columns(uw, um)
     gr[0].wait_recv()
     f0 = [send_rows(10, FL, zh, x3, right)]
@@ -319,87 +343,100 @@
     z.append(send_rows(15, HBR, zh, x2, other))
 
     def local_grads(h, first, last):
-        rows = pl.ds(pl.multiple_of(h * 384, 128), 384)
-
-        @pl.loop(first // 2, last // 2)
-        def _(j):
-            cols = pl.ds(pl.multiple_of(j * 256, 256), 256)
-            gate, upv = gp[rows, cols].astype(F32), up[rows, cols].astype(F32)
-            grad = jnp.concatenate(
-                [hg[2 * j + b, h].reshape(384, 128).astype(F32) for b in range(2)], axis=1
-            )
-            sig = jax.nn.sigmoid(gate)
-            gate_grad = (grad * upv * sig * (1.0 + gate * (1.0 - sig))).astype(BF)
-            up_grad = (grad * gate * sig).astype(BF)
-            for b in range(2):
-                at = slice(b * 128, b * 128 + 128)
-                gg[2 * j + b, h] = gate_grad[:, at].reshape(4, 96, 128)
-                ug[2 * j + b, h] = up_grad[:, at].reshape(4, 96, 128)
-            v = lax.dot_general(gate_grad, gw[:, cols], NT, preferred_element_type=F32)
-            v = v + lax.dot_general(up_grad, uw[:, cols], NT, preferred_element_type=F32)
-            total[h] += v.reshape(4, 2, ROWS, D)
+        @pl.loop(first, last)
+        def _(b):
+            grad = hg[b, h].astype(F32)
+            gg[b, h] = (grad * by_gate[b, h]).astype(BF)
+            ug[b, h] = (grad * by_up[b, h]).astype(BF)
+
+    def product(h, n, first, last):
+        rows, cols = pl.ds(n * COLS, COLS), pl.ds(first * 128, (last - first) * 128)
+
+        def half(grad, w):
+            lhs = jnp.concatenate([grad[b, h].reshape(384, 128) for b in range(first, last)], axis=1)
+            return lax.dot_general(lhs, w[rows, cols], NT, preferred_element_type=F32)
+
+        return (half(gg, gw) + half(ug, uw)).reshape(4, 2, ROWS, COLS)
 
     def write(h, i):
         copies = [
-            pltpu.make_async_copy(gg.at[:, h], gg_out.at[:, h], local.at[1 + i]),
-            pltpu.make_async_copy(ug.at[:, h], ug_out.at[:, h], local.at[2 + i]),
+            pltpu.make_async_copy(gg.at[:, h], gg_out.at[:, h], local.at[5 + i]),
+            pltpu.make_async_copy(ug.at[:, h], ug_out.at[:, h], local.at[6 + i]),
         ]
         for copy in copies:
             copy.start()
         return copies
 
-    r = g + 18
-
-    def to_sibling(h, i):
-        return cp.start(g + 16 + i, total.at[h, :, 1 - c], sib_in.at[i], sibling)
-
-    def piece(h, k, near, q):
-        n = 4 * near + k
+    t = g + 18
+    r = t + 2 * PARTS
+
+    def to_sibling(h, i, n):
+        return cp.start(t + i * PARTS + n, total.at[h, n, :, 1 - c], sib_in.at[i, n], sibling)
+
+    def piece(h, i, n, near, k):
+        z, to = lax.rem(zl + k // 2, 2), y + near + 2 * (k % 2)
+        q = z * 2 + lax.div(lax.rem(to, 4), 2)
+        slot = 4 * near + k
         return pltpu.make_async_remote_copy(
-            src_ref=mine.at[h, q],
-            dst_ref=got.at[n],
-            send_sem=send.at[r + n],
-            recv_sem=recv.at[r + n],
-            device_id=device(x, zh, h, y + k, c),
+            src_ref=mine.at[i, n, q],
+            dst_ref=got.at[slot, n],
+            send_sem=send.at[r + slot * PARTS + n],
+            recv_sem=recv.at[r + slot * PARTS + n],
+            device_id=device(x, zh, z, to, c),
             device_id_type=MESH,
         )
 
-    def spread(h, i, copy):
+    def spread(h, i, n, copy):
         copy.wait_recv()
-        mine[h] = (total[h, :, c] + sib_in[i]).astype(BF)
-        near = lax.rem(h + zl, 2)
+        mine[i, n] = (total[h, n, :, c] + sib_in[i, n]).astype(BF)
+        near = lax.rem(h + y, 2)
 
         @pl.when(near == 1)
         def _():
-            piece(h, 0, near, y).start()
-
-        for k in (1, 3, 2):
-            piece(h, k, near, lax.rem(y + k, 4)).start()
-
-    total[...] = jnp.zeros_like(total)
+            piece(h, i, n, near, 0).start()
+
+        for k in (1, 2, 3):
+            piece(h, i, n, near, k).start()
+
     local_grads(zh, 8, 14)
+    for n in range(PARTS):
+        total[zh, n] = product(zh, n, 8, 14)
     for copy in f0:
         copy.wait_recv()
     local_grads(zh, 0, 8)
-    near = to_sibling(zh, 0)
+    s0 = []
+    for n in range(PARTS):
+        total[zh, n] += product(zh, n, 0, 8)
+        s0.append(to_sibling(zh, 0, n))
+        if n == 1:
+            gr[1].wait_recv()
+            f1 = [send_rows(16, FL, 1 - zh, x3, right)]
+            gl[1].wait_recv()
+            f1.append(send_rows(17, FR, 1 - zh, x1, left))
     writes = write(zh, 0)
-    gr[1].wait_recv()
-    f1 = [send_rows(18 + 8, FL, 1 - zh, x3, right)]
-    gl[1].wait_recv()
-    f1.append(send_rows(18 + 9, FR, 1 - zh, x1, left))
-    spread(zh, 0, near)
+    for n in range(PARTS):
+        spread(zh, 0, n, s0[n])
     for copy in f1 + z:
         copy.wait_recv()
     local_grads(1 - zh, 0, 14)
-    spread(1 - zh, 1, to_sibling(1 - zh, 1))
     writes += write(1 - zh, 2)
-    out_f[...] = total[zl, y, c] + sib_in[lax.rem(zl + zh, 2), y]
-    for n in range(1, 8):
-        wait = piece(lax.rem(zl + n // 4, 2), n % 4, n // 4, y)
-        wait.wait_recv()
-        wait.wait_send()
-        out_f[...] += got[n].astype(F32)
-    out[...] = out_f[...].astype(BF)
+    s1 = []
+    for n in range(PARTS):
+        total[1 - zh, n] = product(1 - zh, n, 0, 14)
+        s1.append(to_sibling(1 - zh, 1, n))
+        if n > 0:
+            spread(1 - zh, 1, n - 1, s1[n - 1])
+    spread(1 - zh, 1, PARTS - 1, s1[PARTS - 1])
+    own_h, own_q = lax.rem(y, 2), zl * 2 + lax.div(y, 2)
+    stage = lax.rem(own_h + zh, 2)
+    for n in range(PARTS):
+        acc = total[own_h, n, own_q, c] + sib_in[stage, n, own_q]
+        for slot in range(1, 8):
+            wait = piece(0, 0, n, slot // 4, slot % 4)
+            wait.wait_recv()
+            wait.wait_send()
+            acc = acc + got[slot, n].astype(F32)
+        out[:, n * COLS : n * COLS + COLS] = acc.astype(BF)
     for copy in writes + [gd, xt_copy]:
         copy.wait()
     cp.finish()
@@ -412,7 +449,7 @@
     blocks = (NC, 2, 4, 96, 128)
     a = pltpu.VMEM((4, 2, 96, 128), BF)
     b = pltpu.VMEM((3, 96, 128), BF)
-    copies = 2 * GATHER + 26 + 18 + 8 + 2
+    copies = 2 * GATHER + 26 + 18 + 10 * PARTS
     return pl.pallas_call(
         main_kernel,
         name="main",
@@ -429,8 +466,8 @@
             pltpu.VMEM((16, ROWS, D), BF),
             pltpu.VMEM((16, ROWS, D), BF),
             pltpu.VMEM((FF, D), BF),
-            pltpu.VMEM((768, FF), BF),
-            pltpu.VMEM((768, FF), BF),
+            pltpu.VMEM((2, 2, 2, 96, FF), BF),
+            pltpu.VMEM((2, 2, 2, 96, FF), BF),
             pltpu.VMEM((D, FF), BF),
             pltpu.VMEM((D, FF), BF),
             pltpu.VMEM(blocks, F32),
@@ -438,7 +475,9 @@
             pltpu.VMEM(blocks, BF),
             pltpu.VMEM(blocks, BF),
             pltpu.VMEM(blocks, BF),
-            pltpu.VMEM((2, 4, 2, ROWS, D), F32),
+            pltpu.VMEM(blocks, F32),
+            pltpu.VMEM(blocks, F32),
+            pltpu.VMEM((2, PARTS, 4, 2, ROWS, COLS), F32),
             pltpu.VMEM((D, 768), BF),
             a, a, a, a, a, a,
             pltpu.VMEM((NA, 2, 96, 128), F32),
@@ -448,13 +487,12 @@
             pltpu.VMEM((6, 4, 96, 128), F32),
             pltpu.VMEM((6, 4, 96, 128), BF),
             b, b, b, b, b, b,
-            pltpu.VMEM((2, 4, ROWS, D), F32),
-            pltpu.VMEM((2, 4, ROWS, D), BF),
-            pltpu.VMEM((8, ROWS, D), BF),
-            pltpu.VMEM((ROWS, D), F32),
+            pltpu.VMEM((2, PARTS, 4, ROWS, COLS), F32),
+            pltpu.VMEM((2, PARTS, 4, ROWS, COLS), BF),
+            pltpu.VMEM((8, PARTS, ROWS, COLS), BF),
             pltpu.SemaphoreType.DMA((copies,)),
             pltpu.SemaphoreType.DMA((copies,)),
-            pltpu.SemaphoreType.DMA((7,)),
+            pltpu.SemaphoreType.DMA((9,)),
         ],
         compiler_params=pltpu.CompilerParams(
             collective_id=0, has_side_effects=True, vmem_limit_bytes=VMEM
@@ -511,7 +549,14 @@
 ):
     masks = (down_mask.T, gate_mask, up_mask)
     gg, ug, xt, gd, grad_input = main(
-        *masks, layer_input, out_grad, gate_pre, up_pre, gate_weight, up_weight, down_weight
+        *masks,
+        layer_input,
+        out_grad,
+        gate_pre.reshape(2, 2, 2, 96, FF),
+        up_pre.reshape(2, 2, 2, 96, FF),
+        gate_weight,
+        up_weight,
+        down_weight,
     )
     grad_gate, grad_up, grad_down = weights(
         *masks, gg.reshape(NC, 768, 128), ug.reshape(NC, 768, 128), xt, gd

time: 99.9 us -> 97.7 us (0.978)
  Pallas kernels: 98.2 us -> 95.8 us
    pallas_call x1, Pallas kernels: 85.2 us -> 82.8 us  [main(): pl.pallas_call(main_kernel, name='main', out_shape=(jax.ShapeDtypeStruct(...]
where the time goes in v3:
time: 97.7 us; the launch traced here: 97.1 us
  Pallas kernels  95.8 us (98%)
    pallas_call x1, Pallas kernels, main(): pl.pallas_call(main_kernel, name='main', out_shape=(jax.ShapeDtypeStruct(...  82.8 us
    pallas_call x1, Pallas kernels, weights(): pl.pallas_call(weights_kernel, name='weights', grid=(FF // 256,), out_sha...  13 us

profile of v3, /device:TPU:1, one launch (start us, length us, event | category | flops | bytes accessed | tf_op | source)
XLA Modules:
  0.0 97.1 jit_solution(2271323929529985836)
XLA Ops:
  0.6 82.8 %main.1 = (bf16[14,2,4,96,128]{4,3,2,1,0:T(8,128)(2,1)}, bf16[14,2,4,96,128]{4,3,2,1,0:T(8,128)(2,1)}, bf16[1024,768]{1,0:T(8,128)(2,1)}, bf16[1792,1024]{1,0:T(8,128)(2,1)}, bf16[48,1024]{1,0:T(8,128)(2,1)}) custom-call(s32[8,14]{1,0:T(8,128)} %bitcast.9, s32[8,14]{1,0:T(8,128)} %gm.3, s32[8,14]{1,0:T(8,128)} %um.3, bf16[48,1024]{1,0:T(8,128)(2,1)} %x_hbm.1, ...), custom_call_target="tpu_custom_call" | custom-call | tf_op jit(solution)/shard_map/main/pallas_call | solution.py:453
  83.4 0.0 copy-start
  83.4 13.0 %weights.1 = (bf16[1024,1792]{1,0:T(8,128)(2,1)}, bf16[1024,1792]{1,0:T(8,128)(2,1)}, bf16[1792,1024]{1,0:T(8,128)(2,1)}) custom-call(s32[8,14]{1,0:T(8,128)} %bitcast.10, s32[8,14]{1,0:T(8,128)} %gm.3, s32[8,14]{1,0:T(8,128)} %um.3, bf16[14,768,128]{2,1,0:T(8,128)(2,1)} %bitcast.5, bf16[14,768,128]{2,1,0:T(8,128)(2,1)} %bitcast.6, ...), custom_call_target="tpu_custom_call" | custom-call | tf_op jit(solution)/shard_map/weights/pallas_call | solution.py:523
  96.4 0.0 copy-done
  96.4 0.6 copy.15
Async XLA Ops:
  83.4 13.0 %copy-start = (bf16[48,1024]{1,0:T(8,128)(2,1)S(1)}, bf16[48,1024]{1,0:T(8,128)(2,1)}, u32[]{:S(2)}) copy-start(bf16[48,1024]{1,0:T(8,128)(2,1)} %get-tuple-element.24) | copy-start | bytes 294916

commit v4 on v3

--- a/solution.py
+++ b/solution.py
@@ -66,6 +66,8 @@
         self.cp, self.base, self.full, self.src, self.own = cp, base, full, src, own
         x, zh, zl, y, c = self.at = coords()
         self.me = full.at[place(zl, y, c)]
+        own.wait()
+        self.src = src = self.me
         self.z = cp.start(base, src, self.me, device(x, zh, 1 - zl, y, c))
         self.n = 7
         self.y1 = [
@@ -98,7 +100,6 @@
         self.step_y(self.y1, self.at[2])
         for copy in [self.sib[0]] + self.sib[2:]:
             copy.wait_recv()
-        self.own.wait()
         self.sib = [self.sib[1]]
 
     def far(self):
@@ -127,13 +128,13 @@
 
 def main_kernel(
     dm, gm, um, x_hbm, og_hbm, gp_hbm, up_hbm, gw_hbm, uw_hbm, dw_hbm,
-    gg_out, ug_out, xt_out, gd_out, out,
+    gate_out, up_out, down_out, out,
     x_full, og_full, dw, gp, up, gw, uw,
     hf, hb, hg, gg, ug, by_gate, by_up, total, xt,
     rl1, rl2, rl3, rr1, rr2, rr3, asum, fa, rz,
     rb, bf, bs, bl1, bl2, bl3, br1, br2, br3,
     sib_in, mine, got,
-    send, recv, local,
+    send, recv, local, stored,
 ):
     x, zh, zl, y, c = coords()
     right, left = device(x + 1, zh, zl, y, c), device(x + 3, zh, zl, y, c)
@@ -157,6 +158,8 @@
 
     cp = Copies(send, recv)
     og = Gather(cp, 0, og_hbm, og_full, own_og)
+    og.step_z()
+    inp = Gather(cp, GATHER, x_hbm, x_full, own_x)
     load_dw.wait()
 
     @pl.loop(0, NC)
@@ -164,15 +167,6 @@
         for k in range(D // 128):
             at = (pl.ds(pl.multiple_of(i * 128, 128), 128), pl.ds(k * 128, 128))
             dw[at] = dw[at] * dm[k, i].astype(F32).astype(BF)
-
-    og.step_z()
-    inp = Gather(cp, GATHER, x_hbm, x_full, own_x)
-    loads = []
-    for i, (src, dst) in enumerate(((gp_hbm, gp), (up_hbm, up))):
-        for h in range(2):
-            loads.append(pltpu.make_async_copy(src.at[:, :, h], dst.at[h], local.at[3 + 2 * i + h]))
-    for load in loads:
-        load.start()
 
     def partial(z, first, last, step):
         @pl.loop(first, last, step=step)
@@ -190,6 +184,12 @@
     og.near()
     partial(zl, 0, 7, 1)
     og.far()
+    loads = []
+    for i, (src, dst) in enumerate(((gp_hbm, gp), (up_hbm, up))):
+        for h in range(2):
+            loads.append(pltpu.make_async_copy(src.at[:, :, h], dst.at[h], local.at[3 + 2 * i + h]))
+    for load in loads:
+        load.start()
 
     B = pl.ds(NA, 6)
     BL, BR = pl.ds(0, 3), pl.ds(3, 3)
@@ -201,9 +201,9 @@
     zb = [
         cp.start(s + i, hb.at[B, 1 - zh, q], rb.at[:, q], other) for i, q in enumerate((x2, x1, x3, x))
     ]
-    a1, a2 = [], []
-    for g in range(2):
-        partial(1 - zl, g, g + 3, 2)
+    a1, a2, a3, za = [], [], [], []
+
+    def open_a(g):
         i = s + 4 + 6 * g
         a1.append(
             (
@@ -211,12 +211,21 @@
                 cp.start(i + 1, hb.at[AR[g], :, x2], rr1.at[GA[g]], left),
             )
         )
+
+    def direct_a(g):
+        i = s + 6 + 6 * g
         a2.append(
             (
-                cp.start(i + 2, hb.at[AR[g], :, x1], rl2.at[GA[g]], right),
-                cp.start(i + 3, hb.at[AL[g], :, x3], rr2.at[GA[g]], left),
+                cp.start(i, hb.at[AR[g], :, x1], rl2.at[GA[g]], right),
+                cp.start(i + 1, hb.at[AL[g], :, x3], rr2.at[GA[g]], left),
             )
         )
+
+    partial(1 - zl, 0, 3, 2)
+    open_a(0)
+    partial(1 - zl, 1, 4, 2)
+    open_a(1)
+    direct_a(0)
     inp.step_z()
     for load in loads:
         load.wait()
@@ -239,11 +248,15 @@
                 at = slice(b * 128, b * 128 + 128)
                 by_gate[2 * j + b] = factor[:, at].reshape(2, 4, 96, 128)
                 by_up[2 * j + b] = gated[:, at].reshape(2, 4, 96, 128)
-            dw[rows, :] = jnp.dot(
+            acc = jnp.dot(
                 hidden.T, og_full[...].reshape(768, D), preferred_element_type=F32
             ).astype(BF)
-
-    a3 = []
+            for a in range(2):
+                for b in range(D // 128):
+                    keep = dm[b, 2 * j + a].astype(F32).astype(BF)
+                    dw[
+                        pl.ds(pl.multiple_of(j * 256 + a * 128, 128), 128), b * 128 : b * 128 + 128
+                    ] = acc[a * 128 : a * 128 + 128, b * 128 : b * 128 + 128] * keep
 
     def turn_a(g):
         a1[g][0].wait_recv()
@@ -258,8 +271,6 @@
         v = add(rb.at[:, q], hf.at[B, zh, q])
         bf[:, q] = v
         bs[:, q] = v.astype(BF)
-
-    za = []
 
     def land_a(g):
         for copy in a2[g] + a3[g]:
@@ -270,31 +281,30 @@
             fa[cols] = asum[cols, 1 - zh].astype(BF)
             za.append(cp.start(s + 16 + 2 * g + k, fa.at[cols], rz.at[cols], other))
 
-    down(0, 2)
+    down(0, 1)
     turn_a(0)
     land_b(0, x2)
     b1r = cp.start(s + 20, bs.at[BL, x2], bl1, right)
     b1l = cp.start(s + 21, bs.at[BR, x2], br1, left)
-    down(2, 3)
     turn_a(1)
+    direct_a(1)
+    down(1, 3)
     land_b(1, x1)
     b2r = cp.start(s + 22, bs.at[BR, x1], bl2, right)
+    land_a(0)
+    land_b(2, x3)
+    b2l = cp.start(s + 24, bs.at[BL, x3], br2, left)
     b1r.wait_recv()
     bl1[...] = add(bl1, bf.at[BL, x1]).astype(BF)
     b3r = cp.start(s + 23, bl1, bl3, right)
-    down(3, 5)
-    land_b(2, x3)
-    b2l = cp.start(s + 24, bs.at[BL, x3], br2, left)
     b1l.wait_recv()
     br1[...] = add(br1, bf.at[BR, x3]).astype(BF)
     b3l = cp.start(s + 25, br1, br3, left)
     inp.near()
-    land_a(0)
+    down(3, 5)
     land_b(3, x)
     land_a(1)
-    down(5, 7)
-    gd = pltpu.make_async_copy(dw, gd_out, local.at[3])
-    gd.start()
+    down(5, 6)
 
     g = s + 26
     A, FL, FR = pl.ds(0, NA), pl.ds(0, 4), pl.ds(4, 4)
@@ -317,9 +327,10 @@
     gr = [send_rows(4, A, zh, x, right)]
     gl = [send_rows(5, A, zh, x, left)]
     inp.far()
+    down(6, 7)
+    gd = pltpu.make_async_copy(dw, down_out, local.at[3])
+    gd.start()
     xt[...] = x_full[...].reshape(768, D).T
-    xt_copy = pltpu.make_async_copy(xt, xt_out, local.at[4])
-    xt_copy.start()
     load_gw.wait()
     mask_columns(gw, gm)
     br.wait_recv()
@@ -358,14 +369,28 @@
 
         return (half(gg, gw) + half(ug, uw)).reshape(4, 2, ROWS, COLS)
 
-    def write(h, i):
-        copies = [
-            pltpu.make_async_copy(gg.at[:, h], gg_out.at[:, h], local.at[5 + i]),
-            pltpu.make_async_copy(ug.at[:, h], ug_out.at[:, h], local.at[6 + i]),
+    def store(j):
+        cols = pl.ds(pl.multiple_of(j * 256, 256), 256)
+        return [
+            pltpu.make_async_copy(gw.at[:, cols], gate_out.at[:, cols], stored.at[0, j]),
+            pltpu.make_async_copy(uw.at[:, cols], up_out.at[:, cols], stored.at[1, j]),
         ]
-        for copy in copies:
-            copy.start()
-        return copies
+
+    def weight_grads(first, last):
+        @pl.loop(first, last)
+        def _(j):
+            for grad, w, mask in ((gg, gw, gm), (ug, uw, um)):
+                rhs = jnp.concatenate([grad[2 * j + b].reshape(768, 128) for b in range(2)], axis=1)
+                acc = jnp.dot(xt[...], rhs, preferred_element_type=F32).astype(BF)
+                for a in range(D // 128):
+                    for b in range(2):
+                        keep = mask[a, 2 * j + b].astype(F32).astype(BF)
+                        w[
+                            a * 128 : a * 128 + 128,
+                            pl.ds(pl.multiple_of(j * 256 + b * 128, 128), 128),
+                        ] = acc[a * 128 : a * 128 + 128, b * 128 : b * 128 + 128] * keep
+            for copy in store(j):
+                copy.start()
 
     t = g + 18
     r = t + 2 * PARTS
@@ -408,25 +433,24 @@
     for n in range(PARTS):
         total[zh, n] += product(zh, n, 0, 8)
         s0.append(to_sibling(zh, 0, n))
-        if n == 1:
-            gr[1].wait_recv()
-            f1 = [send_rows(16, FL, 1 - zh, x3, right)]
-            gl[1].wait_recv()
-            f1.append(send_rows(17, FR, 1 - zh, x1, left))
-    writes = write(zh, 0)
     for n in range(PARTS):
         spread(zh, 0, n, s0[n])
+    gr[1].wait_recv()
+    f1 = [send_rows(16, FL, 1 - zh, x3, right)]
+    gl[1].wait_recv()
+    f1.append(send_rows(17, FR, 1 - zh, x1, left))
     for copy in f1 + z:
         copy.wait_recv()
     local_grads(1 - zh, 0, 14)
-    writes += write(1 - zh, 2)
     s1 = []
     for n in range(PARTS):
         total[1 - zh, n] = product(1 - zh, n, 0, 14)
         s1.append(to_sibling(1 - zh, 1, n))
         if n > 0:
             spread(1 - zh, 1, n - 1, s1[n - 1])
+    weight_grads(0, 1)
     spread(1 - zh, 1, PARTS - 1, s1[PARTS - 1])
+    weight_grads(1, 7)
     own_h, own_q = lax.rem(y, 2), zl * 2 + lax.div(y, 2)
     stage = lax.rem(own_h + zh, 2)
     for n in range(PARTS):
@@ -437,8 +461,10 @@
             wait.wait_send()
             acc = acc + got[slot, n].astype(F32)
         out[:, n * COLS : n * COLS + COLS] = acc.astype(BF)
-    for copy in writes + [gd, xt_copy]:
-        copy.wait()
+    for j in range(7):
+        for copy in store(j):
+            copy.wait()
+    gd.wait()
     cp.finish()
 
 
@@ -454,14 +480,13 @@
         main_kernel,
         name="main",
         out_shape=(
-            jax.ShapeDtypeStruct(blocks, BF),
-            jax.ShapeDtypeStruct(blocks, BF),
-            jax.ShapeDtypeStruct((D, 768), BF),
+            jax.ShapeDtypeStruct((D, FF), BF),
+            jax.ShapeDtypeStruct((D, FF), BF),
             jax.ShapeDtypeStruct((FF, D), BF),
             jax.ShapeDtypeStruct((ROWS, D), BF),
         ),
         in_specs=[smem] * 3 + [hbm] * 7,
-        out_specs=(hbm, hbm, hbm, hbm, vmem),
+        out_specs=(hbm, hbm, hbm, vmem),
         scratch_shapes=[
             pltpu.VMEM((16, ROWS, D), BF),
             pltpu.VMEM((16, ROWS, D), BF),
@@ -492,7 +517,8 @@
             pltpu.VMEM((8, PARTS, ROWS, COLS), BF),
             pltpu.SemaphoreType.DMA((copies,)),
             pltpu.SemaphoreType.DMA((copies,)),
-            pltpu.SemaphoreType.DMA((9,)),
+            pltpu.SemaphoreType.DMA((7,)),
+            pltpu.SemaphoreType.DMA((2, 7)),
         ],
         compiler_params=pltpu.CompilerParams(
             collective_id=0, has_side_effects=True, vmem_limit_bytes=VMEM
@@ -500,39 +526,37 @@
     )(dm, gm, um, layer_input, out_grad, gate_pre, up_pre, gate_weight, up_weight, down_weight)
 
 
-def weights_kernel(dm, gm, um, gg, ug, xt, gd, g_gate, g_up, g_down):
-    j = pl.program_id(0)
-    for grad, out, mask in ((gg, g_gate, gm), (ug, g_up, um)):
-        rhs = jnp.concatenate([grad[0], grad[1]], axis=1)
-        acc = jnp.dot(xt[...], rhs, preferred_element_type=F32)
-        for a in range(D // 128):
-            for b in range(2):
-                at = (slice(a * 128, a * 128 + 128), slice(b * 128, b * 128 + 128))
-                out[at] = (acc[at] * mask[a, 2 * j + b].astype(F32)).astype(BF)
-    for a in range(2):
-        for b in range(D // 128):
-            at = (slice(a * 128, a * 128 + 128), slice(b * 128, b * 128 + 128))
-            g_down[at] = gd[at] * dm[b, 2 * j + a].astype(F32).astype(BF)
-
-
-def weights(dm, gm, um, gg, ug, xt, gd):
-    smem = pl.BlockSpec(memory_space=pltpu.SMEM)
-    cols = pl.BlockSpec((2, 768, 128), lambda j: (j, 0, 0))
-    weight = pl.BlockSpec((D, 256), lambda j: (0, j))
-    down = pl.BlockSpec((256, D), lambda j: (j, 0))
+CHUNKS = 8
+
+
+def deliver_kernel(a, b, d, a_out, b_out, d_out, va, vb, vd, come, go):
+    stages = []
+    for k, (src, via, dst) in enumerate(((a, va, a_out), (b, vb, b_out), (d, vd, d_out))):
+        rows = src.shape[0] // CHUNKS
+        for i in range(CHUNKS):
+            at = pl.ds(i * rows, rows)
+            first = pltpu.make_async_copy(src.at[at], via.at[at], come.at[k, i])
+            first.start()
+            stages.append((first, pltpu.make_async_copy(via.at[at], dst.at[at], go.at[k, i])))
+    for first, second in stages:
+        first.wait()
+        second.start()
+    for _, second in stages:
+        second.wait()
+
+
+def deliver(*grads):
+    hbm = pl.BlockSpec(memory_space=pl.ANY)
     return pl.pallas_call(
-        weights_kernel,
-        name="weights",
-        grid=(FF // 256,),
-        out_shape=(
-            jax.ShapeDtypeStruct((D, FF), BF),
-            jax.ShapeDtypeStruct((D, FF), BF),
-            jax.ShapeDtypeStruct((FF, D), BF),
-        ),
-        in_specs=[smem, smem, smem, cols, cols, pl.BlockSpec((D, 768), lambda j: (0, 0)), down],
-        out_specs=(weight, weight, down),
+        deliver_kernel,
+        name="deliver",
+        out_shape=tuple(jax.ShapeDtypeStruct(g.shape, g.dtype) for g in grads),
+        in_specs=[hbm] * 3,
+        out_specs=(hbm,) * 3,
+        scratch_shapes=[pltpu.VMEM(g.shape, g.dtype) for g in grads]
+        + [pltpu.SemaphoreType.DMA((3, CHUNKS))] * 2,
         compiler_params=pltpu.CompilerParams(vmem_limit_bytes=VMEM),
-    )(dm, gm, um, gg, ug, xt, gd)
+    )(*grads)
 
 
 def shards(
@@ -548,7 +572,7 @@
     down_mask,
 ):
     masks = (down_mask.T, gate_mask, up_mask)
-    gg, ug, xt, gd, grad_input = main(
+    grad_gate, grad_up, grad_down, grad_input = main(
         *masks,
         layer_input,
         out_grad,
@@ -558,10 +582,7 @@
         up_weight,
         down_weight,
     )
-    grad_gate, grad_up, grad_down = weights(
-        *masks, gg.reshape(NC, 768, 128), ug.reshape(NC, 768, 128), xt, gd
-    )
-    return (grad_input, grad_gate, grad_up, grad_down)
+    return (grad_input, *deliver(grad_gate, grad_up, grad_down))
 
 
 def solution(mesh):

time: 97.7 us -> 95.6 us (0.979)
  Pallas kernels: 95.8 us -> 94.1 us
    pallas_call x1, Pallas kernels: 13 us -> 8.37 us  [deliver(): pl.pallas_call(deliver_kernel, name='deliver', out_shape=tuple((jax.Shape...]
    pallas_call x1, Pallas kernels: 82.8 us -> 85.8 us  [main(): pl.pallas_call(main_kernel, name='main', out_shape=(jax.ShapeDtypeStruct(...]
where the time goes in v4:
time: 95.6 us; the launch traced here: 95.5 us
  Pallas kernels  94.1 us (98%)
    pallas_call x1, Pallas kernels, main(): pl.pallas_call(main_kernel, name='main', out_shape=(jax.ShapeDtypeStruct(...  85.8 us
    pallas_call x1, Pallas kernels, deliver(): pl.pallas_call(deliver_kernel, name='deliver', out_shape=tuple((jax.Shape...  8.37 us

profile of v4, /device:TPU:1, one launch (start us, length us, event | category | flops | bytes accessed | tf_op | source)
XLA Modules:
  0.0 95.5 jit_solution(13265024574504440077)
XLA Ops:
  0.6 85.8 %main.1 = (bf16[1024,1792]{1,0:T(8,128)(2,1)}, bf16[1024,1792]{1,0:T(8,128)(2,1)}, bf16[1792,1024]{1,0:T(8,128)(2,1)}, bf16[48,1024]{1,0:T(8,128)(2,1)}) custom-call(s32[8,14]{1,0:T(8,128)} %bitcast.5, s32[8,14]{1,0:T(8,128)} %gm.1, s32[8,14]{1,0:T(8,128)} %um.1, bf16[48,1024]{1,0:T(8,128)(2,1)} %x_hbm.1, bf16[48,1024]{1,0:T(8,128)(2,1)} %og_hbm.1, ...), custom_call_target="tpu_custom_call" | custom-call | tf_op jit(solution)/shard_map/main/pallas_call | solution.py:479
  86.4 0.0 copy-start
  86.4 8.4 %deliver.1 = (bf16[1024,1792]{1,0:T(8,128)(2,1)}, bf16[1024,1792]{1,0:T(8,128)(2,1)}, bf16[1792,1024]{1,0:T(8,128)(2,1)}) custom-call(bf16[1024,1792]{1,0:T(8,128)(2,1)} %get-tuple-element.12.a, bf16[1024,1792]{1,0:T(8,128)(2,1)} %get-tuple-element.13.b, bf16[1792,1024]{1,0:T(8,128)(2,1)} %get-tuple-element.14.d), custom_call_target="tpu_custom_call" | custom-call | tf_op jit(solution)/shard_map/deliver/pallas_call | solution.py:550
  94.8 0.0 copy-done
  94.8 0.6 copy.15
Async XLA Ops:
  86.4 8.4 %copy-start = (bf16[48,1024]{1,0:T(8,128)(2,1)S(1)}, bf16[48,1024]{1,0:T(8,128)(2,1)}, u32[]{:S(2)}) copy-start(bf16[48,1024]{1,0:T(8,128)(2,1)} %get-tuple-element.22) | copy-start | bytes 294916

commit v5 on v4

--- a/solution.py
+++ b/solution.py
@@ -15,7 +15,7 @@
 NC = 14
 GATHER = 15
 VMEM = 63 * 1024 * 1024
-PARTS = 4
+PARTS = 2
 COLS = D // PARTS
 
 
@@ -71,7 +71,7 @@
         self.z = cp.start(base, src, self.me, device(x, zh, 1 - zl, y, c))
         self.n = 7
         self.y1 = [
-            cp.start(base + k, src, self.me, device(x, zh, zl, y + k, c)) for k in (1, 3, 2)
+            cp.start(base + k, src, self.me, device(x, zh, zl, y + k, c)) for k in (2, 1, 3)
         ]
         self.sib = [cp.start(base + 7, src, self.me, device(x, zh, zl, y, 1 - c))]
 
@@ -86,24 +86,28 @@
         self.z.wait_recv()
         piece = self.full.at[place(1 - zl, y, c)]
         self.y2 = [
-            self.cp.start(self.base + 3 + k, piece, piece, device(x, zh, zl, y + k, c)) for k in (1, 3, 2)
+            self.cp.start(self.base + 3 + k, piece, piece, device(x, zh, zl, y + k, c)) for k in (1, 3)
         ]
         self.to_sibling(place(1 - zl, y, c))
 
-    def step_y(self, copies, z):
+    def near(self):
         x, zh, zl, y, c = self.at
-        for copy, k in zip(copies, (1, 3, 2)):
+        for copy, k in zip(self.y1, (2, 1, 3)):
             copy.wait_recv()
-            self.to_sibling(place(z, y + 4 - k, c))
-
-    def near(self):
-        self.step_y(self.y1, self.at[2])
+            r = place(zl, y + 4 - k, c)
+            if k == 2:
+                piece = self.full.at[r]
+                self.z2 = self.cp.start(self.base + 5, piece, piece, device(x, zh, 1 - zl, y, c))
+            self.to_sibling(r)
         for copy in [self.sib[0]] + self.sib[2:]:
             copy.wait_recv()
         self.sib = [self.sib[1]]
 
     def far(self):
-        self.step_y(self.y2, 1 - self.at[2])
+        x, zh, zl, y, c = self.at
+        for copy, k in zip([self.z2] + self.y2, (2, 1, 3)):
+            copy.wait_recv()
+            self.to_sibling(place(1 - zl, y + 4 - k, c))
         for copy in self.sib:
             copy.wait_recv()
 
@@ -195,7 +199,8 @@
     BL, BR = pl.ds(0, 3), pl.ds(3, 3)
     HBL, HBR = pl.ds(NA, 3), pl.ds(NA + 3, 3)
     GA = (pl.ds(0, 2), pl.ds(2, 2))
-    AL, AR = GA, (pl.ds(4, 2), pl.ds(6, 2))
+    AL, AR = (pl.ds(0, 2), pl.ds(4, 2)), (pl.ds(2, 2), pl.ds(6, 2))
+    AG = (pl.ds(0, 4), pl.ds(4, 4))
     s = 2 * GATHER
     partial(1 - zl, 4, 7, 1)
     zb = [
@@ -221,9 +226,9 @@
             )
         )
 
-    partial(1 - zl, 0, 3, 2)
+    partial(1 - zl, 0, 2, 1)
     open_a(0)
-    partial(1 - zl, 1, 4, 2)
+    partial(1 - zl, 2, 4, 1)
     open_a(1)
     direct_a(0)
     inp.step_z()
@@ -277,9 +282,9 @@
             copy.wait_recv()
         asum[AL[g]] = add(hf.at[AL[g], :, x], rl3.at[GA[g]], rr2.at[GA[g]])
         asum[AR[g]] = add(hf.at[AR[g], :, x], rr3.at[GA[g]], rl2.at[GA[g]])
-        for k, cols in enumerate((AL[g], AR[g])):
-            fa[cols] = asum[cols, 1 - zh].astype(BF)
-            za.append(cp.start(s + 16 + 2 * g + k, fa.at[cols], rz.at[cols], other))
+        cols = AG[g]
+        fa[cols] = asum[cols, 1 - zh].astype(BF)
+        za.append(cp.start(s + 16 + g, fa.at[cols], rz.at[cols], other))
 
     down(0, 1)
     turn_a(0)
@@ -353,12 +358,13 @@
     fl.wait_recv()
     z.append(send_rows(15, HBR, zh, x2, other))
 
-    def local_grads(h, first, last):
+    def local_grads(h, q, first=0, last=NC):
         @pl.loop(first, last)
         def _(b):
-            grad = hg[b, h].astype(F32)
-            gg[b, h] = (grad * by_gate[b, h]).astype(BF)
-            ug[b, h] = (grad * by_up[b, h]).astype(BF)
+            at = (b, h) if q is None else (b, h, q)
+            grad = hg[at].astype(F32)
+            gg[at] = (grad * by_gate[at]).astype(BF)
+            ug[at] = (grad * by_up[at]).astype(BF)
 
     def product(h, n, first, last):
         rows, cols = pl.ds(n * COLS, COLS), pl.ds(first * 128, (last - first) * 128)
@@ -423,12 +429,12 @@
         for k in (1, 2, 3):
             piece(h, i, n, near, k).start()
 
-    local_grads(zh, 8, 14)
+    local_grads(zh, None, 8, 14)
     for n in range(PARTS):
         total[zh, n] = product(zh, n, 8, 14)
     for copy in f0:
         copy.wait_recv()
-    local_grads(zh, 0, 8)
+    local_grads(zh, None, 0, 8)
     s0 = []
     for n in range(PARTS):
         total[zh, n] += product(zh, n, 0, 8)
@@ -439,9 +445,13 @@
     f1 = [send_rows(16, FL, 1 - zh, x3, right)]
     gl[1].wait_recv()
     f1.append(send_rows(17, FR, 1 - zh, x1, left))
-    for copy in f1 + z:
+    for copy in z[:3]:
         copy.wait_recv()
-    local_grads(1 - zh, 0, 14)
+    for q in (x, x1, x3):
+        local_grads(1 - zh, q)
+    for copy in f1 + z[3:]:
+        copy.wait_recv()
+    local_grads(1 - zh, x2)
     s1 = []
     for n in range(PARTS):
         total[1 - zh, n] = product(1 - zh, n, 0, 14)

time: 95.6 us -> 89.8 us (0.939); the launches traced: 95.5 us -> 88.1 us
  Pallas kernels: 94.1 us -> 86.8 us
    pallas_call x1, Pallas kernels: 85.8 us -> 78.4 us  [main(): pl.pallas_call(main_kernel, name='main', out_shape=(jax.ShapeDtypeStruct(...]
where the time goes in v5:
time: 89.8 us; the launch traced here: 88.1 us
  Pallas kernels  86.8 us (97%)
    pallas_call x1, Pallas kernels, main(): pl.pallas_call(main_kernel, name='main', out_shape=(jax.ShapeDtypeStruct(...  78.4 us
    pallas_call x1, Pallas kernels, deliver(): pl.pallas_call(deliver_kernel, name='deliver', out_shape=tuple((jax.Shape...  8.37 us

profile of v5, /device:TPU:1, one launch (start us, length us, event | category | flops | bytes accessed | tf_op | source)
XLA Modules:
  0.0 88.1 jit_solution(11937805795863037103)
XLA Ops:
  0.6 78.4 %main.1 = (bf16[1024,1792]{1,0:T(8,128)(2,1)}, bf16[1024,1792]{1,0:T(8,128)(2,1)}, bf16[1792,1024]{1,0:T(8,128)(2,1)}, bf16[48,1024]{1,0:T(8,128)(2,1)}) custom-call(s32[8,14]{1,0:T(8,128)} %bitcast.5, s32[8,14]{1,0:T(8,128)} %gm.1, s32[8,14]{1,0:T(8,128)} %um.1, bf16[48,1024]{1,0:T(8,128)(2,1)} %x_hbm.1, bf16[48,1024]{1,0:T(8,128)(2,1)} %og_hbm.1, ...), custom_call_target="tpu_custom_call" | custom-call | tf_op jit(solution)/shard_map/main/pallas_call | solution.py:489
  79.1 0.0 copy-start
  79.1 8.4 %deliver.1 = (bf16[1024,1792]{1,0:T(8,128)(2,1)}, bf16[1024,1792]{1,0:T(8,128)(2,1)}, bf16[1792,1024]{1,0:T(8,128)(2,1)}) custom-call(bf16[1024,1792]{1,0:T(8,128)(2,1)} %get-tuple-element.12.a, bf16[1024,1792]{1,0:T(8,128)(2,1)} %get-tuple-element.13.b, bf16[1792,1024]{1,0:T(8,128)(2,1)} %get-tuple-element.14.d), custom_call_target="tpu_custom_call" | custom-call | tf_op jit(solution)/shard_map/deliver/pallas_call | solution.py:560
  87.5 0.0 copy-done
  87.5 0.6 copy.15
Async XLA Ops:
  79.1 8.4 %copy-start = (bf16[48,1024]{1,0:T(8,128)(2,1)S(1)}, bf16[48,1024]{1,0:T(8,128)(2,1)}, u32[]{:S(2)}) copy-start(bf16[48,1024]{1,0:T(8,128)(2,1)} %get-tuple-element.22) | copy-start | bytes 294916

commit v6 on v5

--- a/solution.py
+++ b/solution.py
@@ -439,12 +439,12 @@
     for n in range(PARTS):
         total[zh, n] += product(zh, n, 0, 8)
         s0.append(to_sibling(zh, 0, n))
-    for n in range(PARTS):
-        spread(zh, 0, n, s0[n])
     gr[1].wait_recv()
     f1 = [send_rows(16, FL, 1 - zh, x3, right)]
     gl[1].wait_recv()
     f1.append(send_rows(17, FR, 1 - zh, x1, left))
+    for n in range(PARTS):
+        spread(zh, 0, n, s0[n])
     for copy in z[:3]:
         copy.wait_recv()
     for q in (x, x1, x3):

time: 89.8 us -> 89.9 us (level)
  the two profiles are of different devices: /device:TPU:1 before, /device:TPU:8 now
where the time goes in v6:
time: 89.9 us; the launch traced here: 89.7 us
  Pallas kernels  88.4 us (98%)
    pallas_call x1, Pallas kernels, main(): pl.pallas_call(main_kernel, name='main', out_shape=(jax.ShapeDtypeStruct(...  80 us
    pallas_call x1, Pallas kernels, deliver(): pl.pallas_call(deliver_kernel, name='deliver', out_shape=tuple((jax.Shape...  8.37 us

profile of v6, /device:TPU:8, one launch (start us, length us, event | category | flops | bytes accessed | tf_op | source)
XLA Modules:
  0.0 89.7 jit_solution(17745529063244859499)
XLA Ops:
  0.6 80.0 %main.1 = (bf16[1024,1792]{1,0:T(8,128)(2,1)}, bf16[1024,1792]{1,0:T(8,128)(2,1)}, bf16[1792,1024]{1,0:T(8,128)(2,1)}, bf16[48,1024]{1,0:T(8,128)(2,1)}) custom-call(s32[8,14]{1,0:T(8,128)} %bitcast.5, s32[8,14]{1,0:T(8,128)} %gm.1, s32[8,14]{1,0:T(8,128)} %um.1, bf16[48,1024]{1,0:T(8,128)(2,1)} %x_hbm.1, bf16[48,1024]{1,0:T(8,128)(2,1)} %og_hbm.1, ...), custom_call_target="tpu_custom_call" | custom-call | tf_op jit(solution)/shard_map/main/pallas_call | solution.py:489
  80.7 0.0 copy-start
  80.7 8.4 %deliver.1 = (bf16[1024,1792]{1,0:T(8,128)(2,1)}, bf16[1024,1792]{1,0:T(8,128)(2,1)}, bf16[1792,1024]{1,0:T(8,128)(2,1)}) custom-call(bf16[1024,1792]{1,0:T(8,128)(2,1)} %get-tuple-element.12.a, bf16[1024,1792]{1,0:T(8,128)(2,1)} %get-tuple-element.13.b, bf16[1792,1024]{1,0:T(8,128)(2,1)} %get-tuple-element.14.d), custom_call_target="tpu_custom_call" | custom-call | tf_op jit(solution)/shard_map/deliver/pallas_call | solution.py:560
  89.1 0.0 copy-done
  89.1 0.6 copy.15
Async XLA Ops:
  80.7 8.4 %copy-start = (bf16[48,1024]{1,0:T(8,128)(2,1)S(1)}, bf16[48,1024]{1,0:T(8,128)(2,1)}, u32[]{:S(2)}) copy-start(bf16[48,1024]{1,0:T(8,128)(2,1)} %get-tuple-element.22) | copy-start | bytes 294916
